TPU v7x, 128 devices: a whole 4x4x4 slice. The times are simulated.
128 devices in a mesh: row: 8 (over x_lo, y), col: 16 (over z, x_hi, core).
Axes of the slice: x: 4 (x_hi: 2, x_lo: 2; x = x_hi * 2 + x_lo), y: 4, z: 4, core: 2. Of those that a mesh axis runs over, the one named last changes fastest.
Arguments:
- features: bfloat16 [65536, 256], P(('row', 'col')), may hold values from -6 to 6
- weight: bfloat16 [256, 256], replicated, may hold values from -0.375 to 0.375
- adjacency: bfloat16 [8, 16, 384, 128, 128], P('row', 'col'), may hold values from -0.0546875 to 0.0546875
- block_rows: int32 [8, 16, 384], P('row', 'col'), may hold values from 0 to 63
- block_cols: int32 [8, 16, 384], P('row', 'col'), may hold values from 0 to 31
- live_blocks: int32 [8, 16], P('row', 'col'), may hold values from 96 to 384, as said below
- part_gains: float32 [64, 256], replicated, may hold values from 0.5 to 2
- partition: int32 [65536], P(('row', 'col')), may hold values from 0 to 63, never falling along the last dimension, each value on 1 to 2048 neighbouring positions
- cotangent: bfloat16 [65536, 256], P(('row', 'col')), may hold values from -6 to 6
Outputs:
- layer_out: bfloat16 [65536, 256], P(('row', 'col'))
- feature_grad: bfloat16 [65536, 256], P(('row', 'col'))
- weight_grad: float32 [256, 256], replicated
- gain_grad: float32 [64, 256], replicated
Inputs may be any that keep to these rules, and one draw needn't show every extreme that they name: Only the first live_blocks[i, j] slots of tile (i, j) are used; some tile uses all 384 slots. partition numbers never fall along the nodes; every partition has 1 to 2048 nodes, one exactly that many.
All inputs are finite; a program needn't handle non-finite values.
Results may differ from a plain program's by a relative error of at most 0.024.
Values may be sent and summed in bfloat16 or wider, within the bound.
A program may use at most 128 MiB of HBM per device.

v0:
```python
import math

import jax
import jax.numpy as jnp
from jax import lax
from jax.sharding import PartitionSpec as P

BLOCK = 128


def silu_slope(values):
    sig = jax.nn.sigmoid(values)
    return sig * (1.0 + values * (1.0 - sig))


def tile_sum(tile_values, row_index, col_index, live_count, panels, out_blocks, forward):
    slot_count = tile_values.shape[0]
    group_size = math.gcd(slot_count, 64)
    feature_width = panels.shape[1]
    panel_blocks = panels.reshape(-1, BLOCK, feature_width)
    group_count = (live_count + group_size - 1) // group_size

    def one_group(position, totals):
        first_slot = position * group_size
        values_here = lax.dynamic_slice_in_dim(tile_values, first_slot, group_size, 0)
        rows_here = lax.dynamic_slice_in_dim(row_index, first_slot, group_size, 0)
        cols_here = lax.dynamic_slice_in_dim(col_index, first_slot, group_size, 0)
        slot_mask = (first_slot + jnp.arange(group_size, dtype=jnp.int32) < live_count).astype(
            jnp.float32
        )
        if forward:
            products = jnp.einsum(
                "kab,kbf->kaf",
                values_here,
                panel_blocks[cols_here],
                preferred_element_type=jnp.float32,
            )
            targets = rows_here
        else:
            products = jnp.einsum(
                "kab,kaf->kbf",
                values_here,
                panel_blocks[rows_here],
                preferred_element_type=jnp.float32,
            )
            targets = cols_here
        return totals.at[targets].add(products * slot_mask[:, None, None])

    start_totals = jnp.zeros((out_blocks, BLOCK, feature_width), jnp.float32)
    totals = lax.fori_loop(0, group_count, one_group, start_totals)
    return totals.reshape(out_blocks * BLOCK, feature_width)


def per_device(
    features,
    weight,
    adjacency,
    block_rows,
    block_cols,
    live_blocks,
    part_gains,
    partition,
    cotangent,
):
    node_count = features.shape[0]
    live_count = live_blocks[0, 0]
    tile_values = adjacency[0, 0]
    row_index = block_rows[0, 0]
    col_index = block_cols[0, 0]
    hidden = jnp.dot(features, weight, preferred_element_type=jnp.float32).astype(jnp.bfloat16)
    panels = lax.all_gather(hidden, "row", axis=0, tiled=True)
    member = (
        partition[:, None] == jnp.arange(part_gains.shape[0], dtype=jnp.int32)[None, :]
    ).astype(jnp.float32)
    row_gains = jnp.dot(member, part_gains, precision=lax.Precision.HIGHEST)
    upstream = cotangent.astype(jnp.float32) * row_gains
    partial_rows = tile_sum(
        tile_values,
        row_index,
        col_index,
        live_count,
        panels,
        node_count * lax.axis_size("col") // BLOCK,
        True,
    )
    summed = lax.psum_scatter(
        partial_rows.astype(jnp.bfloat16), "col", scatter_dimension=0, tiled=True
    ).astype(jnp.float32)
    local_grad = (upstream * silu_slope(summed)).astype(jnp.bfloat16)
    agg_grad = lax.all_gather(local_grad, "col", axis=0, tiled=True)
    activated = jax.nn.silu(summed)
    layer_out = (activated * row_gains).astype(jnp.bfloat16)
    partial_cols = tile_sum(
        tile_values,
        row_index,
        col_index,
        live_count,
        agg_grad,
        node_count * lax.axis_size("row") // BLOCK,
        False,
    )
    hidden_grad = lax.psum_scatter(
        partial_cols.astype(jnp.bfloat16), "row", scatter_dimension=0, tiled=True
    )
    feature_grad = lax.dot_general(
        hidden_grad, weight, (((1,), (1,)), ((), ())), preferred_element_type=jnp.float32
    ).astype(jnp.bfloat16)
    weight_part = lax.dot_general(
        features, hidden_grad, (((0,), (0,)), ((), ())), preferred_element_type=jnp.float32
    )
    part_terms = jnp.dot(
        member.T, cotangent.astype(jnp.float32) * activated, precision=lax.Precision.HIGHEST
    )
    part_sizes = jnp.sum(member, axis=0)
    weight_total, part_total, size_total = lax.psum(
        (weight_part, part_terms, part_sizes), ("row", "col")
    )
    total_nodes = node_count * lax.axis_size("row") * lax.axis_size("col")
    weight_grad = weight_total / jnp.sqrt(jnp.float32(total_nodes))
    gain_grad = part_total / jnp.sqrt(size_total)[:, None]
    return (layer_out, feature_grad, weight_grad, gain_grad)


def solution(mesh):
    in_specs = (
        P(("row", "col"), None),
        P(),
        P("row", "col", None, None, None),
        P("row", "col", None),
        P("row", "col", None),
        P("row", "col"),
        P(),
        P(("row", "col")),
        P(("row", "col"), None),
    )
    out_specs = (P(("row", "col"), None), P(("row", "col"), None), P(), P())
    return jax.shard_map(
        per_device, mesh=mesh, in_specs=in_specs, out_specs=out_specs, check_vma=False
    )
```

profile of v0, /device:TPU:1, one launch (start us, length us, event | category | flops | bytes accessed | tf_op | source)
XLA Modules:
  0.0 808.1 jit_solution(6598130624264618743)
XLA Ops:
  7.2 0.9 copy-done
  8.1 1.8 convolution_convert_fusion.1
  10.7 0.7 reduce
  11.4 0.7 reduce.1
  12.1 37.6 %all-gather.3.cloned.1.call-done = bf16[4096,256]{1,0:T(8,128)(2,1)} async-done(((bf16[512,256]{1,0:T(8,128)(2,1)}), bf16[4096,256]{1,0:T(8,128)(2,1)}) %all-gather.3.cloned.1.call-update) | async-done | bytes 2097168 | tf_op jit(solution)/shard_map/all_gather | solution.py:71
  49.7 4.3 broadcast_in_dim.23
  54.0 120.9 %while.20 = (s32[]{:T(128)}, f32[64,128,256]{2,1,0:T(8,128)}, s32[]{:T(128)}, s32[384]{0:T(512)S(1)}, bf16[384,128,128]{2,1,0:T(8,128)(2,1)}, /*index=5*/s32[384...) while((s32[]{:T(128)}, f32[64,128,256]{2,1,0:T(8,128)}, ...), condition=%wide.region_2.3_spmd, body=%wide.region_0.2_spmd.sunk | while | flops 541066816 | bytes 48241072 | solution.py:50
  54.0 0.6 compare_convert_fusion.4
  54.7 0.1 compare_select_fusion.6
  54.7 2.7 gather_fusion
  57.5 7.3 broadcast_multiply_fusion.5
  64.8 19.5 %scatter_fusion = f32[64,128,256]{2,1,0:T(8,128)} fusion(f32[64,128,256]{2,1,0:T(8,128)} %get-tuple-element.277, s32[64]{0:T(128)S(1)} %get-tuple-element.252, f32[64,128,256]{2,1,0:T(8,128)} %broadcast_multiply_fusion.5), kind=kCustom, calls=%fused_computation.2.clone.1 | custom fusion | flops 2097152 | bytes 25166080 | tf_op jit(solution)/shard_map/while/body/scatter-add | solution.py:47
  84.3 0.6 compare_convert_fusion.4
  84.9 0.1 compare_select_fusion.6
  85.0 2.7 gather_fusion
  87.7 7.3 broadcast_multiply_fusion.5
  95.0 19.5 %scatter_fusion = f32[64,128,256]{2,1,0:T(8,128)} fusion(f32[64,128,256]{2,1,0:T(8,128)} %get-tuple-element.277, s32[64]{0:T(128)S(1)} %get-tuple-element.252, f32[64,128,256]{2,1,0:T(8,128)} %broadcast_multiply_fusion.5), kind=kCustom, calls=%fused_computation.2.clone.1 | custom fusion | flops 2097152 | bytes 25166080 | tf_op jit(solution)/shard_map/while/body/scatter-add | solution.py:47
  114.5 0.6 compare_convert_fusion.4
  115.2 0.1 compare_select_fusion.6
  115.3 2.7 gather_fusion
  118.0 7.3 broadcast_multiply_fusion.5
  125.3 19.6 %scatter_fusion = f32[64,128,256]{2,1,0:T(8,128)} fusion(f32[64,128,256]{2,1,0:T(8,128)} %get-tuple-element.277, s32[64]{0:T(128)S(1)} %get-tuple-element.252, f32[64,128,256]{2,1,0:T(8,128)} %broadcast_multiply_fusion.5), kind=kCustom, calls=%fused_computation.2.clone.1 | custom fusion | flops 2097152 | bytes 25166080 | tf_op jit(solution)/shard_map/while/body/scatter-add | solution.py:47
  144.9 0.6 compare_convert_fusion.4
  145.5 0.1 compare_select_fusion.6
  145.6 2.7 gather_fusion
  148.3 7.3 broadcast_multiply_fusion.5
  155.6 19.3 %scatter_fusion = f32[64,128,256]{2,1,0:T(8,128)} fusion(f32[64,128,256]{2,1,0:T(8,128)} %get-tuple-element.277, s32[64]{0:T(128)S(1)} %get-tuple-element.252, f32[64,128,256]{2,1,0:T(8,128)} %broadcast_multiply_fusion.5), kind=kCustom, calls=%fused_computation.2.clone.1 | custom fusion | flops 2097152 | bytes 25166080 | tf_op jit(solution)/shard_map/while/body/scatter-add | solution.py:47
  174.9 5.9 convert_element_type.49
  180.9 143.9 %reduce-scatter.3.cloned.1.call-done = bf16[512,256]{1,0:T(8,128)(2,1)} async-done(((bf16[8192,256]{1,0:T(8,128)(2,1)}), bf16[512,256]{1,0:T(8,128)(2,1)}) %reduce-scatter.3.cloned.1.call-update) | async-done | bytes 262160 | tf_op jit(solution)/shard_map/reduce_scatter | solution.py:86
  324.9 2.3 fusion.5
  327.2 16.6 %copy.16 = bf16[1,1,384,128,128]{3,4,2,1,0:T(8,128)(2,1)} copy(bf16[1,1,384,128,128]{4,3,2,1,0:T(8,128)(2,1)} %bitcast.26) | data formatting | bytes 25165824 | tf_op args[2]
  343.9 40.4 %all-gather.5.cloned.1.call-done = bf16[8192,256]{1,0:T(8,128)(2,1)} async-done(((bf16[512,256]{1,0:T(8,128)(2,1)}), bf16[8192,256]{1,0:T(8,128)(2,1)}) %all-gather.5.cloned.1.call-update) | async-done | bytes 4194320 | tf_op jit(solution)/shard_map/all_gather | solution.py:90
  384.2 2.4 broadcast_in_dim.24
  386.7 129.1 %while.21 = (s32[]{:T(128)}, f32[32,128,256]{2,1,0:T(8,128)}, s32[]{:T(128)}, s32[384]{0:T(512)S(1)}, bf16[384,128,128]{1,2,0:T(8,128)(2,1)}, /*index=5*/s32[384...) while((s32[]{:T(128)}, f32[32,128,256]{2,1,0:T(8,128)}, ...), condition=%wide.region_6.7_spmd, body=%wide.region_4.6_spmd.sunk | while | flops 541066816 | bytes 48241072 | solution.py:50
  386.7 0.6 compare_convert_fusion.5
  387.3 0.1 compare_select_fusion.7
  387.4 5.0 gather_fusion.1
  392.4 7.3 broadcast_multiply_fusion.6
  399.6 19.4 %scatter_fusion.1 = f32[32,128,256]{2,1,0:T(8,128)} fusion(f32[32,128,256]{2,1,0:T(8,128)} %get-tuple-element.313, s32[64]{0:T(128)S(1)} %get-tuple-element.262, f32[64,128,256]{2,1,0:T(8,128)} %broadcast_multiply_fusion.6), kind=kCustom, calls=%fused_computation.3.clone.1 | custom fusion | flops 2097152 | bytes 25166080 | tf_op jit(solution)/shard_map/while/body/scatter-add | solution.py:47
  419.1 0.6 compare_convert_fusion.5
  419.7 0.1 compare_select_fusion.7
  419.8 5.0 gather_fusion.1
  424.8 7.3 broadcast_multiply_fusion.6
  432.0 19.3 %scatter_fusion.1 = f32[32,128,256]{2,1,0:T(8,128)} fusion(f32[32,128,256]{2,1,0:T(8,128)} %get-tuple-element.313, s32[64]{0:T(128)S(1)} %get-tuple-element.262, f32[64,128,256]{2,1,0:T(8,128)} %broadcast_multiply_fusion.6), kind=kCustom, calls=%fused_computation.3.clone.1 | custom fusion | flops 2097152 | bytes 25166080 | tf_op jit(solution)/shard_map/while/body/scatter-add | solution.py:47
  451.3 0.6 compare_convert_fusion.5
  452.0 0.1 compare_select_fusion.7
  452.1 5.0 gather_fusion.1
  457.0 7.3 broadcast_multiply_fusion.6
  464.3 19.2 %scatter_fusion.1 = f32[32,128,256]{2,1,0:T(8,128)} fusion(f32[32,128,256]{2,1,0:T(8,128)} %get-tuple-element.313, s32[64]{0:T(128)S(1)} %get-tuple-element.262, f32[64,128,256]{2,1,0:T(8,128)} %broadcast_multiply_fusion.6), kind=kCustom, calls=%fused_computation.3.clone.1 | custom fusion | flops 2097152 | bytes 25166080 | tf_op jit(solution)/shard_map/while/body/scatter-add | solution.py:47
  483.5 0.6 compare_convert_fusion.5
  484.2 0.1 compare_select_fusion.7
  484.3 5.0 gather_fusion.1
  489.2 7.3 broadcast_multiply_fusion.6
  496.5 19.3 %scatter_fusion.1 = f32[32,128,256]{2,1,0:T(8,128)} fusion(f32[32,128,256]{2,1,0:T(8,128)} %get-tuple-element.313, s32[64]{0:T(128)S(1)} %get-tuple-element.262, f32[64,128,256]{2,1,0:T(8,128)} %broadcast_multiply_fusion.6), kind=kCustom, calls=%fused_computation.3.clone.1 | custom fusion | flops 2097152 | bytes 25166080 | tf_op jit(solution)/shard_map/while/body/scatter-add | solution.py:47
  515.7 3.9 convert_element_type.55
  519.7 0.1 convert_reduce_fusion
  519.8 135.0 %psum.23 = f32[64]{0:T(128)S(1)} all-reduce(f32[64]{0:T(128)S(1)} %convert_reduce_fusion), channel_id=1, replica_groups=mesh['row'=8,'col'=16] {'row','col'}, use_global_device_ids=true, to_apply=%region_11.12 | all-reduce | flops 64 | bytes 512 | tf_op jit(solution)/shard_map/psum | solution.py:115
  654.8 1.1 fusion.6
  655.9 1.9 convolution_bitcast_fusion
  657.9 1.9 convolution_convert_fusion
  659.8 138.4 %all-reduce.3.cloned.1.call-done = (f32[256,256]{0,1:T(8,128)}, f32[64,256]{1,0:T(8,128)}) async-done(((f32[256,256]{0,1:T(8,128)}, f32[64,256]{1,0:T(8,128)}), (f32[256,256]{0,1:T(8,128)}, f32[64,256]{1,0:T(8,128)})) %all-reduce.3.cloned.1.call-update) | async-done | bytes 327696 | tf_op jit(solution)/shard_map/psum | solution.py:115
  798.2 1.0 broadcast_multiply_fusion.2
  799.2 0.8 copy.18
  800.0 1.5 broadcast_divide_fusion
  (33 shorter events, 0.4 us)
Async XLA Ops:
  7.2 1.0 copy-start
  7.2 42.6 %all-gather.3.cloned.1.call-start = ((), (), s32[]{:S(2)}) async-start(), calls=%async_computation.2 | async-start | bytes 2359296 | tf_op jit(solution)/shard_map/all_gather | solution.py:71
  10.0 314.9 %reduce-scatter.3.cloned.1.call-start = ((), (), s32[]{:S(2)}) async-start(), calls=%async_computation.3 | async-start | bytes 4456448 | tf_op jit(solution)/shard_map/reduce_scatter | solution.py:86
  49.7 4.3 copy-start.1
  180.9 144.0 %copy-start.3 = (s32[512]{0:T(512)S(1)}, s32[512]{0:T(512)}, u32[]{:S(2)}) copy-start(s32[512]{0:T(512)} %param.20) | copy-start | bytes 6148
  180.9 144.0 %copy-start.4 = (bf16[512,256]{1,0:T(8,128)(2,1)S(1)}, bf16[512,256]{1,0:T(8,128)(2,1)}, u32[]{:S(2)}) copy-start(bf16[512,256]{1,0:T(8,128)(2,1)} %param.21) | copy-start | bytes 786436
  180.9 144.0 %copy-start.6 = (f32[64,256]{1,0:T(8,128)S(1)}, f32[64,256]{1,0:T(8,128)}, u32[]{:S(2)}) copy-start(f32[64,256]{1,0:T(8,128)} %param.19) | copy-start | bytes 196612
  180.9 203.4 %all-gather.5.cloned.1.call-start = ((), (), s32[]{:S(2)}) async-start(), calls=%async_computation.4 | async-start | bytes 4456448 | tf_op jit(solution)/shard_map/all_gather | solution.py:90
  327.2 328.8 %reduce-scatter.5.cloned.1.call-start = ((), (), s32[]{:S(2)}) async-start(), calls=%async_computation.5 | async-start | bytes 2359296 | tf_op jit(solution)/shard_map/reduce_scatter | solution.py:102
  515.7 139.1 %copy-start.5 = (bf16[512,256]{1,0:T(8,128)(2,1)S(1)}, bf16[512,256]{1,0:T(8,128)(2,1)}, u32[]{:S(2)}) copy-start(bf16[512,256]{1,0:T(8,128)(2,1)} %reduce-scatter.3.cloned.1.call-done) | copy-start | bytes 786436
  519.6 138.3 %copy-start.2 = (bf16[256,256]{1,0:T(8,128)(2,1)S(1)}, bf16[256,256]{1,0:T(8,128)(2,1)}, u32[]{:S(2)}) copy-start(bf16[256,256]{1,0:T(8,128)(2,1)} %param.14) | copy-start | bytes 393220
  519.6 278.5 %all-reduce.3.cloned.1.call-start = ((), (), s32[]{:S(2)}) async-start(), calls=%async_computation.6 | async-start | bytes 655360 | tf_op jit(solution)/shard_map/psum | solution.py:115
Sparse Core Ops, SparseCore 0:
  10.2 39.4 all-gather.2
  181.0 143.7 reduce-scatter.2
  328.2 55.9 all-gather.4
  519.8 98.8 reduce-scatter.4
  658.0 140.1 all-reduce.2
where the time goes:
time: 810 us; the launch traced here: 808 us
  waiting for transfers between devices  360 us (44%)
  other arithmetic  175 us (22%)
  blocking collectives  135 us (17%)
  matrix products  67.3 us (8%)
  local copies, waits for them, and re-layouts  55.9 us (7%)
  between operations  14.5 us (2%)
    scatter-add x8, other arithmetic, one_group(): return totals.at[targets].add(products * slot_mask[:, None, None])  155 us
    reduce_scatter x1, waiting for transfers between devices, per_device(): lax.psum_scatter(partial_rows.astype(jnp.bfloat16), 'col', scatter_dimens...  144 us
    psum x1, waiting for transfers between devices, per_device(): lax.psum((weight_part, part_terms, part_sizes), ('row', 'col'))  138 us
    psum x1, blocking collectives, per_device(): lax.psum((weight_part, part_terms, part_sizes), ('row', 'col'))  135 us
    all_gather x1, waiting for transfers between devices, per_device(): agg_grad = lax.all_gather(local_grad, 'col', axis=0, tiled=True)  40.4 us
    all_gather x1, waiting for transfers between devices, per_device(): panels = lax.all_gather(hidden, 'row', axis=0, tiled=True)  37.6 us
    dot_general x4, matrix products, one_group(): jnp.einsum('kab,kbf->kaf', values_here, panel_blocks[cols_here], preferre...  29.2 us
    dot_general x4, matrix products, one_group(): jnp.einsum('kab,kaf->kbf', values_here, panel_blocks[rows_here], preferre...  29 us
  transfers between devices with their start and end apart: 5, of which 4 were waited for; matrix products, arithmetic and copies ran while one was open for 3% of the time, Pallas kernels for 0%

commit v1 on v0

v1 whole, which is shorter than its diff:
```python
import jax
import jax.numpy as jnp
from jax import lax
from jax.experimental import pallas as pl
from jax.experimental.pallas import tpu as pltpu
from jax.sharding import PartitionSpec as P

BLOCK = 128
SLOTS = 384
WIDTH = 256
CHUNKS = 2
LANES = 128
PARTS = 64
NODES = 65536
UNROLL = 16
MESH = pl.DeviceIdType.MESH
F32 = jnp.float32
BF16 = jnp.bfloat16


def order_slots(target, other, live_count, count, order):
    slot = jnp.arange(SLOTS, dtype=jnp.int32)
    key = jnp.where(slot < live_count, target, count)
    mark = key * 512 + slot
    rank = jnp.sum((mark[None, :] < mark[:, None]).astype(jnp.int32), axis=1)
    packed = (slot * 128 + key) * 128 + other
    hit = rank[None, :] == slot[:, None]
    ranked = jnp.sum(jnp.where(hit, packed[None, :], 0), axis=1)
    sorted_key = (ranked // 128) % 128
    keep = jnp.concatenate([jnp.zeros((1,), F32), (sorted_key[1:] == sorted_key[:-1]).astype(F32)])
    upto = jnp.sum((key[None, :] <= order[:, None]).astype(jnp.int32), axis=1)
    some = jnp.any(key[None, :] == order[:, None], axis=1)
    last = jnp.where(some, upto - 1, SLOTS)
    return ranked // (128 * 128), ranked % 128, keep, last


def silu_parts(v):
    g = 1.0 / (1.0 + jnp.exp(-v))
    return v * g, g * (1.0 + v * (1.0 - g))


def kernel(
    perm_f, idx_f, keep_f, last_f, perm_b, idx_b, keep_b, last_b,
    x_ref, w_ref, a_hbm, pg_ref, part_ref, cot_ref,
    lo_ref, fg_ref, wg_ref, gg_ref,
    a_v, s_v, h0, h1, r0, r1, cx0, cx1, t0, t1, zr0, zr1, ux0, ux1, xr0, xr1,
    g0, g1, p0, p1, yr0, yr1, vx0, vx1, vr0, vr1,
    wp0, wp1, wr0, wr1, ws0, ws1, wc0, wc1, wf0, wf1,
    rg_v, mt_v, xt_v, hg_v,
    a_sem, send, recv,
):
    row = lax.axis_index("row")
    col = lax.axis_index("col")
    xl, y = row // 4, row % 4
    z, xh, core = col // 4, (col // 2) % 2, col % 2

    def at(xl=xl, y=y, z=z, xh=xh, core=core):
        return (xl * 4 + y, z * 4 + xh * 2 + core)

    H, R, CX, T, ZR = (h0, h1), (r0, r1), (cx0, cx1), (t0, t1), (zr0, zr1)
    UX, XR, G, PP, YR = (ux0, ux1), (xr0, xr1), (g0, g1), (p0, p1), (yr0, yr1)
    VX, VR = (vx0, vx1), (vr0, vr1)
    WP, WR, WS, WC, WF = (wp0, wp1), (wr0, wr1), (ws0, ws1), (wc0, wc1), (wf0, wf1)

    started = []

    def push(src, dst, device):
        n = len(started)
        copy = pltpu.make_async_remote_copy(
            src_ref=src, dst_ref=dst, send_sem=send.at[n], recv_sem=recv.at[n],
            device_id=device, device_id_type=MESH,
        )
        copy.start()
        started.append(copy)
        return copy

    pieces = 4
    step = SLOTS // pieces
    loads = [
        pltpu.make_async_copy(
            a_hbm.at[pl.ds(n * step, step)], a_v.at[pl.ds(n * step, step)], a_sem.at[n]
        )
        for n in range(pieces)
    ]
    for load in loads:
        load.start()

    barrier = pltpu.get_barrier_semaphore()
    for d in range(1, 8):
        pl.semaphore_signal(barrier, inc=1, device_id=((row + d) % 8, col), device_id_type=MESH)
    for d in range(1, 16):
        pl.semaphore_signal(barrier, inc=1, device_id=(row, (col + d) % 16), device_id_type=MESH)

    own_h = pl.ds(row * 4, 4)
    for c in range(CHUNKS):
        hidden = jnp.dot(x_ref[...], w_ref[:, c * LANES:(c + 1) * LANES], preferred_element_type=F32)
        H[c][own_h] = hidden.astype(BF16).reshape(4, BLOCK, LANES)
    pl.semaphore_wait(barrier, 22)

    ag_x, ag_y = {}, {}

    def gather_x(c):
        mine = H[c].at[own_h]
        ag_x[c] = push(mine, mine, at(xl=1 - xl))

    def gather_y_own(c):
        mine = H[c].at[own_h]
        ag_y[c] = [push(mine, mine, at(y=(y + d) % 4)) for d in (1, 3, 2)]

    def gather_y_other(c):
        ag_x[c].wait_recv()
        other = H[c].at[pl.ds(((1 - xl) * 4 + y) * 4, 4)]
        ag_y[c] += [push(other, other, at(y=(y + d) % 4)) for d in (1, 3, 2)]

    def tile_pass(c, forward, first, stop, acc):
        perm, idx, keep = (perm_f, idx_f, keep_f) if forward else (perm_b, idx_b, keep_b)

        def body(t, acc):
            for u in range(UNROLL):
                k = t * UNROLL + u
                block = a_v[perm[k]]
                panel = (H if forward else G)[c][idx[k]]
                if forward:
                    term = jnp.dot(block, panel, preferred_element_type=F32)
                else:
                    term = jnp.dot(panel, block, preferred_element_type=F32)
                acc = acc * keep[k] + term
                s_v[k] = acc.astype(BF16)
            return acc

        return lax.fori_loop(first // UNROLL, stop // UNROLL, body, acc)

    def collect(dst, last, count):
        def body(q, carry):
            for u in range(8):
                dst[q * 8 + u] = s_v[last[q * 8 + u]]
            return carry

        lax.fori_loop(0, count // 8, body, 0)

    zero = jnp.zeros((BLOCK, LANES), F32)

    def core_send(c):
        return push(R[c].at[pl.ds((1 - core) * 32, 32)], CX[c], at(core=1 - core))

    def core_add(c, copy):
        copy.wait_recv()

        def body(b, carry):
            T[c][b] = (R[c][core * 32 + b].astype(F32) + CX[c][b].astype(F32)).astype(BF16)
            return carry

        lax.fori_loop(0, 32, body, 0)

    def z_send(c):
        return [
            push(T[c].at[pl.ds(((z + d) % 4) * 8, 8)], ZR[c].at[d - 1], at(z=(z + d) % 4))
            for d in (1, 3, 2)
        ]

    def z_sum(c, which):
        rows = pl.ds(z * 8 + which * 4, 4)
        total = T[c][rows].astype(F32)
        for d in range(3):
            total = total + ZR[c][d, pl.ds(which * 4, 4)].astype(F32)
        return total

    def x_send(c, copies):
        for copy in copies:
            copy.wait_recv()
        UX[c][...] = z_sum(c, 1 - xh).astype(BF16)
        return push(UX[c], XR[c], at(xh=1 - xh))

    def slot_of(zz, xx, cc):
        return pl.ds(cc * 32 + (zz * 2 + xx) * 4, 4)

    def activate(c, copy):
        copy.wait_recv()
        lanes = slice(c * LANES, (c + 1) * LANES)
        summed = (z_sum(c, xh) + XR[c][...].astype(F32)).reshape(4 * BLOCK, LANES)
        act, slope = silu_parts(summed)
        gains = rg_v[:, lanes]
        cot = cot_ref[:, lanes].astype(F32)
        grad = cot * gains * slope
        for b in range(4):
            G[c][core * 32 + (z * 2 + xh) * 4 + b] = grad[b * BLOCK:(b + 1) * BLOCK].T.astype(BF16)
        return act, gains, cot

    def after_activate(c, held):
        act, gains, cot = held
        lanes = slice(c * LANES, (c + 1) * LANES)
        lo_ref[:, lanes] = (act * gains).astype(BF16)
        terms = jnp.dot(mt_v[...], cot * act, precision=lax.Precision.HIGHEST, preferred_element_type=F32)
        sizes = jnp.dot(
            mt_v[...], jnp.ones((4 * BLOCK, LANES), F32), preferred_element_type=F32
        )
        for i in range(8):
            WP[c][i, 32:40] = terms[i * 8:(i + 1) * 8]
            WP[c][i, 40:48] = sizes[i * 8:(i + 1) * 8]

    def grad_send(c):
        mine = G[c].at[slot_of(z, xh, core)]
        first = push(mine, mine, at(xh=1 - xh))
        zs = [push(mine, mine, at(z=(z + d) % 4)) for d in (1, 3, 2)]
        return first, zs, [push(mine, mine, at(core=1 - core))]

    def grad_forward(c, state):
        first, zs, cores = state
        first.wait_recv()
        other = G[c].at[slot_of(z, 1 - xh, core)]
        zs2 = [push(other, other, at(z=(z + d) % 4)) for d in (1, 3, 2)]
        cores.append(push(other, other, at(core=1 - core)))
        return zs, zs2, cores

    def grad_finish(c, state):
        zs, zs2, cores = state
        for xx, group in ((xh, zs), (1 - xh, zs2)):
            for d, copy in zip((1, 3, 2), group):
                copy.wait_recv()
                got = G[c].at[slot_of((z + 4 - d) % 4, xx, core)]
                cores.append(push(got, got, at(core=1 - core)))
        for copy in cores:
            copy.wait_recv()

    def y_send(c):
        return [
            push(PP[c].at[pl.ds(((y + d) % 4) * 8, 8)], YR[c].at[d - 1], at(y=(y + d) % 4))
            for d in (1, 3, 2)
        ]

    def y_sum(c, which):
        total = PP[c][pl.ds(y * 8 + which * 4, 4)].astype(F32)
        for d in range(3):
            total = total + YR[c][d, pl.ds(which * 4, 4)].astype(F32)
        return total

    def x2_send(c, copies):
        for copy in copies:
            copy.wait_recv()
        VX[c][...] = y_sum(c, 1 - xl).astype(BF16)
        return push(VX[c], VR[c], at(xl=1 - xl))

    def finish_hidden(c, copy):
        copy.wait_recv()
        lanes = slice(c * LANES, (c + 1) * LANES)
        total = y_sum(c, xl) + VR[c][...].astype(F32)
        for b in range(4):
            hg_v[b * BLOCK:(b + 1) * BLOCK, lanes] = total[b].T.astype(BF16)
        part = jnp.dot(xt_v[...], hg_v[:, lanes], preferred_element_type=F32)
        for i in range(8):
            WP[c][i, 0:32] = part[i * 32:(i + 1) * 32]
        return [
            push(WP[c].at[(row + d) % 8], WR[c].at[d - 1], ((row + d) % 8, col))
            for d in range(1, 8)
        ]

    def weight_cols(c, copies):
        total = WP[c][row]
        for d, copy in enumerate(copies):
            copy.wait_recv()
            total = total + WR[c][d]
        WS[c][...] = total
        return [
            push(WS[c], WC[c].at[d - 1], (row, (col + d) % 16)) for d in range(1, 16)
        ]

    def weight_rows(c, copies):
        total = jnp.zeros((48, LANES), F32)
        for copy in copies:
            copy.wait_recv()
        WC[c][15] = WS[c][...]
        for j in range(16):
            total = total + WC[c][(col + 15 - j) % 16]
        WF[c][row, 0:32] = total[0:32] / 256.0
        WF[c][row, 32:48] = total[32:48]
        mine = WF[c].at[row]
        return [push(mine, mine, ((row + d) % 8, col)) for d in range(1, 8)]

    def weight_out(c, copies):
        for copy in copies:
            copy.wait_recv()
        lanes = slice(c * LANES, (c + 1) * LANES)
        for i in range(8):
            wg_ref[i * 32:(i + 1) * 32, lanes] = WF[c][i, 0:32]
            gg_ref[i * 8:(i + 1) * 8, lanes] = WF[c][i, 32:40] / jnp.sqrt(WF[c][i, 40:48])

    gather_x(0)
    gather_y_own(0)
    gather_x(1)
    s_v[SLOTS] = jnp.zeros((BLOCK, LANES), BF16)
    gather_y_other(0)
    ids = lax.broadcasted_iota(jnp.int32, (PARTS, 4 * BLOCK), 0)
    mt_v[...] = (part_ref[...] == ids).astype(F32)
    rg_v[...] = lax.dot_general(
        mt_v[...], pg_ref[...], (((0,), (0,)), ((), ())),
        precision=lax.Precision.HIGHEST, preferred_element_type=F32,
    )
    xt_v[...] = x_ref[...].astype(F32).T.astype(BF16)
    for load in loads:
        load.wait()
    for copy in ag_y[0]:
        copy.wait_recv()
    gather_y_own(1)
    gather_y_other(1)

    tile_pass(0, True, 0, SLOTS, zero)
    collect(R[0], last_f, 64)
    cs0 = core_send(0)
    for copy in ag_y[1]:
        copy.wait_recv()
    acc = tile_pass(1, True, 0, 128, zero)
    core_add(0, cs0)
    zs0 = z_send(0)
    tile_pass(1, True, 128, SLOTS, acc)
    collect(R[1], last_f, 64)
    cs1 = core_send(1)
    xs0 = x_send(0, zs0)
    core_add(1, cs1)
    zs1 = z_send(1)
    held = activate(0, xs0)
    gs0 = grad_send(0)
    after_activate(0, held)
    gs0 = grad_forward(0, gs0)
    xs1 = x_send(1, zs1)
    held = activate(1, xs1)
    gs1 = grad_send(1)
    after_activate(1, held)
    gs1 = grad_forward(1, gs1)
    grad_finish(0, gs0)
    tile_pass(0, False, 0, SLOTS, zero)
    collect(PP[0], last_b, 32)
    ys0 = y_send(0)
    grad_finish(1, gs1)
    tile_pass(1, False, 0, SLOTS, zero)
    collect(PP[1], last_b, 32)
    vs0 = x2_send(0, ys0)
    ys1 = y_send(1)
    wr0_ = finish_hidden(0, vs0)
    wc0_ = weight_cols(0, wr0_)
    wf0_ = weight_rows(0, wc0_)
    vs1 = x2_send(1, ys1)
    wr1_ = finish_hidden(1, vs1)
    fg_ref[...] = lax.dot_general(
        hg_v[...], w_ref[...], (((1,), (1,)), ((), ())), preferred_element_type=F32
    ).astype(BF16)
    wc1_ = weight_cols(1, wr1_)
    weight_out(0, wf0_)
    wf1_ = weight_rows(1, wc1_)
    weight_out(1, wf1_)
    for copy in started:
        copy.wait_send()


def per_device(
    features, weight, adjacency, block_rows, block_cols, live_blocks, part_gains, partition, cotangent
):
    live = live_blocks[0, 0]
    rows, cols = block_rows[0, 0], block_cols[0, 0]
    place = jnp.arange(64, dtype=jnp.int32)
    row_order = ((place % 32) // 4 * 2 + place // 32) * 4 + place % 4
    spot = jnp.arange(32, dtype=jnp.int32)
    col_order = ((spot // 4 % 2) * 4 + spot // 8) * 4 + spot % 4
    row_place = (rows // 4 % 2) * 32 + (rows // 8) * 4 + rows % 4
    forward = order_slots(rows, cols, live, 64, row_order)
    backward = order_slots(cols, row_place, live, 32, col_order)

    nodes = features.shape[0]
    smem = pl.BlockSpec(memory_space=pltpu.SMEM)
    vmem = pl.BlockSpec(memory_space=pltpu.VMEM)
    hbm = pl.BlockSpec(memory_space=pl.ANY)

    def pair(shape, dtype=BF16):
        return [pltpu.VMEM(shape, dtype)] * 2

    tile = (BLOCK, LANES)
    copies = 2 * (1 + 3 + 3 + 1 + 3 + 1 + 5 + 4 + 6 + 3 + 1 + 7 + 15 + 7)
    outs = (
        jax.ShapeDtypeStruct((nodes, WIDTH), BF16),
        jax.ShapeDtypeStruct((nodes, WIDTH), BF16),
        jax.ShapeDtypeStruct((WIDTH, WIDTH), F32),
        jax.ShapeDtypeStruct((PARTS, WIDTH), F32),
    )
    return pl.pallas_call(
        kernel,
        out_shape=outs,
        in_specs=[smem] * 8 + [vmem, vmem, hbm, vmem, vmem, vmem],
        out_specs=(vmem,) * 4,
        scratch_shapes=[
            pltpu.VMEM((SLOTS,) + tile, BF16),
            pltpu.VMEM((SLOTS + 1,) + tile, BF16),
            *pair((32,) + tile), *pair((64,) + tile), *pair((32,) + tile), *pair((32,) + tile),
            *pair((3, 8) + tile), *pair((4,) + tile), *pair((4,) + tile),
            *pair((64,) + tile), *pair((32,) + tile), *pair((3, 8) + tile),
            *pair((4,) + tile), *pair((4,) + tile),
            *pair((8, 48, LANES), F32), *pair((7, 48, LANES), F32), *pair((48, LANES), F32),
            *pair((16, 48, LANES), F32), *pair((8, 48, LANES), F32),
            pltpu.VMEM((nodes, WIDTH), F32),
            pltpu.VMEM((PARTS, nodes), F32),
            pltpu.VMEM((WIDTH, nodes), BF16),
            pltpu.VMEM((nodes, WIDTH), BF16),
            pltpu.SemaphoreType.DMA((4,)),
            pltpu.SemaphoreType.DMA((copies,)),
            pltpu.SemaphoreType.DMA((copies,)),
        ],
        compiler_params=pltpu.CompilerParams(
            collective_id=0, has_side_effects=True, vmem_limit_bytes=60 * 2**20
        ),
    )(
        *forward, *backward,
        features, weight, adjacency[0, 0], part_gains, partition.reshape(1, nodes), cotangent,
    )


def solution(mesh):
    in_specs = (
        P(("row", "col"), None),
        P(),
        P("row", "col", None, None, None),
        P("row", "col", None),
        P("row", "col", None),
        P("row", "col"),
        P(),
        P(("row", "col")),
        P(("row", "col"), None),
    )
    out_specs = (P(("row", "col"), None), P(("row", "col"), None), P(), P())
    return jax.shard_map(
        per_device, mesh=mesh, in_specs=in_specs, out_specs=out_specs, check_vma=False
    )
```

time: 810 us -> 166 us (0.20)
  waiting for transfers between devices: 360 us -> 0 us
  other arithmetic: 175 us -> 6.57 us
  Pallas kernels: 0 us -> 151 us
  blocking collectives: 135 us -> 0 us
  matrix products: 67.3 us -> 0 us
  local copies, waits for them, and re-layouts: 55.9 us -> 6.48 us
  between operations: 14.5 us -> 1.32 us
    scatter-add x8 -> x0, other arithmetic: 155 us -> none  [one_group(): return totals.at[targets].add(products * slot_mask[:, None, None])]
    pallas_call x0 -> x1, Pallas kernels: none -> 151 us  [per_device(): pl.pallas_call(kernel, out_shape=outs, in_specs=[smem] * 8 + [vmem, vmem,...]
    reduce_scatter x2 -> x0, waiting for transfers between devices: 144 us -> none  [the longest x1 144 us: per_device(): lax.psum_scatter(partial_rows.astype(jnp.bfloat16), 'col', scatter_dimens...]
    psum x1 -> x0, waiting for transfers between devices: 138 us -> none  [per_device(): lax.psum((weight_part, part_terms, part_sizes), ('row', 'col'))]
    psum x1 -> x0, blocking collectives: 135 us -> none  [per_device(): lax.psum((weight_part, part_terms, part_sizes), ('row', 'col'))]
    all_gather x2 -> x0, waiting for transfers between devices: 78 us -> none  [the longest x1 40.4 us: per_device(): agg_grad = lax.all_gather(local_grad, 'col', axis=0, tiled=True)]
    dot_general x13 -> x0, matrix products: 67.3 us -> none  [the longest x4 29.2 us: one_group(): jnp.einsum('kab,kbf->kaf', values_here, panel_blocks[cols_here], preferre...]
    gather x8 -> x0, local copies, waits for them, and re-layouts: 30.8 us -> none  [the longest x4 19.8 us: one_group(): panel_blocks[rows_here]]
  transfers between devices with their start and end apart: 5 -> 0, of which waited for: 4 -> 0; matrix products, arithmetic and copies ran while one was open for 3% -> 0% of each run, Pallas kernels for 0% -> 0%
where the time goes in v1:
time: 166 us
  Pallas kernels  151 us (91%)
  other arithmetic  6.57 us (4%)
  local copies, waits for them, and re-layouts  6.48 us (4%)
    pallas_call x1, Pallas kernels, per_device(): pl.pallas_call(kernel, out_shape=outs, in_specs=[smem] * 8 + [vmem, vmem,...  151 us
    unnamed x4, local copies, waits for them, and re-layouts  6.48 us

profile of v1, /device:TPU:1, one launch (start us, length us, event | category | flops | bytes accessed | tf_op | source)
XLA Modules:
  0.0 165.7 jit_solution(18330650121824874719)
XLA Ops:
  1.3 0.7 reduce.1
  2.0 0.7 reduce
  2.7 0.2 convert_reduce_fusion
  2.9 0.2 compare_reduce_fusion.1
  3.1 0.2 convert_reduce_fusion.3
  3.3 0.6 add_select_fusion.12.last_b
  3.9 0.3 select_reduce_fusion
  4.2 0.2 select_reduce_fusion.1
  4.4 0.2 compare_reduce_fusion
  4.5 0.2 convert_reduce_fusion.2
  4.7 0.5 add_select_fusion.13.last_f
  5.2 0.6 add_select_fusion.8
  5.8 0.1 slice_compare_fusion.1
  5.9 0.7 fusion.13.keep_f
  6.6 0.6 add_select_fusion
  7.2 0.1 slice_compare_fusion
  7.2 0.7 fusion.14.keep_b
  7.9 151.3 %shard_map.120 = (bf16[512,256]{1,0:T(8,128)(2,1)}, bf16[512,256]{1,0:T(8,128)(2,1)}, f32[256,256]{1,0:T(8,128)}, f32[64,256]{1,0:T(8,128)}) custom-call(s32[384]{0:T(512)} %get-tuple-element.13.perm_f, s32[384]{0:T(512)} %get-tuple-element.14.idx_f, f32[384]{0:T(512)} %fusion.13.keep_f, s32[64]{0:T(128)} %add_select_fusion.13.last_f, ...), custom_call_target="tpu_custom_call" | custom-call | tf_op jit(solution)/shard_map/pallas_call | solution.py:383
  159.2 1.7 %copy.18 = bf16[512,256]{1,0:T(8,128)(2,1)} copy(bf16[512,256]{1,0:T(8,128)(2,1)} %get-tuple-element.21) | data formatting | bytes 524288
  160.8 1.7 %copy.19 = bf16[512,256]{1,0:T(8,128)(2,1)} copy(bf16[512,256]{1,0:T(8,128)(2,1)} %get-tuple-element.22) | data formatting | bytes 524288
  162.5 1.7 %copy.20 = f32[256,256]{1,0:T(8,128)} copy(f32[256,256]{1,0:T(8,128)} %get-tuple-element.23) | data formatting | bytes 524288
  164.2 1.5 copy.21
  (5 shorter events, 0.1 us)

commit v2 on v1

v2 whole, which is shorter than its diff:
```python
import jax
import jax.numpy as jnp
from jax import lax
from jax.experimental import pallas as pl
from jax.experimental.pallas import tpu as pltpu
from jax.sharding import PartitionSpec as P

BLOCK = 128
SLOTS = 384
WIDTH = 256
CHUNKS = 2
LANES = 128
PARTS = 64
NODES = 65536
UNROLL = 32
MESH = pl.DeviceIdType.MESH
F32 = jnp.float32
BF16 = jnp.bfloat16


def order_slots(target, other, live_count, count, order):
    slot = lax.broadcasted_iota(jnp.int32, (1, SLOTS), 1)

    def column(row):
        return jnp.broadcast_to(row, (LANES, SLOTS)).T

    def wide(tall):
        return jnp.concatenate([tall] * (SLOTS // LANES), axis=1)

    def total(flags):
        return jnp.sum(flags.astype(jnp.int32), axis=0, keepdims=True)

    key = jnp.where(slot < live_count, target, count)
    mark = key * 512 + slot
    key_col = column(key)
    mark_col = wide(column(mark))
    rank = total(mark_col < mark)
    below = total(mark_col < key * 512)
    keep = (rank != below).astype(jnp.int32)
    entry = wide(column((slot * 64 + other) * 2 + keep))
    hit = wide(column(rank)) == slot
    entries = jnp.sum(jnp.where(hit, entry, 0), axis=0, keepdims=True)
    upto = total(key_col <= order)
    some = total(key_col == order)
    return entries, jnp.where(some > 0, upto - 1, SLOTS)


def silu_parts(v):
    g = 1.0 / (1.0 + jnp.exp(-v))
    return v * g, g * (1.0 + v * (1.0 - g))


def kernel(
    rows_ref, cols_ref, live_ref, x_ref, w_ref, a_hbm, pg_ref, part_ref, cot_ref,
    lo_ref, fg_ref, wg_ref, gg_ref,
    table_v, table, a_v, s_v, h0, h1, r0, r1, cx0, cx1, t0, t1, g0, g1, p0, p1,
    ca0, ca1, cp0, cp1, cm0, cm1, cb0, cb1, cs0_, cs1_, cl0, cl1,
    ra0, ra1, rp0, rp1, rm0, rm1, rb0, rb1, rs0_, rs1_, rl0, rl1,
    wp0, wp1, wr0, wr1, ws0, ws1, wc0, wc1, wf0, wf1,
    rg_v, mt_v, xt_v, hg_v,
    a_sem, t_sem, send, recv,
):
    row = lax.axis_index("row")
    col = lax.axis_index("col")
    xl, y = row // 4, row % 4
    z, xh, core = col // 4, (col // 2) % 2, col % 2

    def at(xl=xl, y=y, z=z, xh=xh, core=core):
        return (xl * 4 + y, z * 4 + xh * 2 + core)

    H, R, CX, T, G, PP = (h0, h1), (r0, r1), (cx0, cx1), (t0, t1), (g0, g1), (p0, p1)
    COL = ((ca0, cp0, cm0, cb0, cs0_, cl0), (ca1, cp1, cm1, cb1, cs1_, cl1))
    ROW = ((ra0, rp0, rm0, rb0, rs0_, rl0), (ra1, rp1, rm1, rb1, rs1_, rl1))
    WP, WR, WS, WC, WF = (wp0, wp1), (wr0, wr1), (ws0, ws1), (wc0, wc1), (wf0, wf1)

    started = []

    def push(src, dst, device):
        n = len(started)
        copy = pltpu.make_async_remote_copy(
            src_ref=src, dst_ref=dst, send_sem=send.at[n], recv_sem=recv.at[n],
            device_id=device, device_id_type=MESH,
        )
        copy.start()
        started.append(copy)
        return copy

    def arrive(copies):
        for copy in copies:
            copy.wait_recv()

    pieces = 4
    step = SLOTS // pieces
    loads = [
        pltpu.make_async_copy(
            a_hbm.at[pl.ds(n * step, step)], a_v.at[pl.ds(n * step, step)], a_sem.at[n]
        )
        for n in range(pieces)
    ]

    barrier = pltpu.get_barrier_semaphore()
    for d in range(1, 8):
        pl.semaphore_signal(barrier, inc=1, device_id=((row + d) % 8, col), device_id_type=MESH)
    for d in range(1, 16):
        pl.semaphore_signal(barrier, inc=1, device_id=(row, (col + d) % 16), device_id_type=MESH)

    own_h = pl.ds(row * 4, 4)
    for c in range(CHUNKS):
        hidden = jnp.dot(x_ref[...], w_ref[:, c * LANES:(c + 1) * LANES], preferred_element_type=F32)
        H[c][own_h] = hidden.astype(BF16).reshape(4, BLOCK, LANES)
    pl.semaphore_wait(barrier, 22)

    row_ring, row_pair = (lambda d: at(y=(y + d) % 4)), at(xl=1 - xl)
    col_ring, col_pair = (lambda d: at(z=(z + d) % 4)), at(xh=1 - xh)
    hops = (1, 3, 2)

    def gather_pair(buf, slot_of, ring, pair, to_pair):
        mine = buf.at[pl.ds(slot_of(ring, pair), 4)]
        return push(mine, mine, to_pair)

    def gather_ring(buf, slot_of, ring, pair, to_ring):
        mine = buf.at[pl.ds(slot_of(ring, pair), 4)]
        return [push(mine, mine, to_ring(d)) for d in hops]

    def gather_on_pair(buf, slot_of, ring, pair, to_ring, pair_copy):
        pair_copy.wait_recv()
        other = buf.at[pl.ds(slot_of(ring, 1 - pair), 2)]
        return [push(other, other, to_ring(d)) for d in hops]

    def gather_on_ring(buf, slot_of, ring, pair, to_pair, ring_copies):
        out = []
        for d, copy in zip(hops, ring_copies):
            copy.wait_recv()
            got = buf.at[pl.ds(slot_of((ring + 4 - d) % 4, pair) + 2, 2)]
            out.append(push(got, got, to_pair))
        return out

    def row_slot(ring, pair):
        return (pair * 4 + ring) * 4

    def col_slot(ring, pair):
        return core * 32 + (ring * 2 + pair) * 4

    def sum_start(bufs, src, ring, pair, to_ring, to_pair):
        b_pair = push(src.at[pl.ds(16 + (1 - pair) * 8, 8)], bufs[1], to_pair)
        a_ring = [
            push(src.at[pl.ds(((ring + d) % 4) * 4, 4)], bufs[0].at[d - 1], to_ring(d)) for d in hops
        ]
        return b_pair, a_ring

    def sum_on_pair(bufs, src, ring, pair, to_ring, b_pair):
        b_pair.wait_recv()
        bufs[2][...] = (
            src[pl.ds(16 + pair * 8, 8)].astype(F32) + bufs[1][...].astype(F32)
        ).astype(BF16)
        return [
            push(bufs[2].at[pl.ds(((ring + d) % 4) * 2, 2)], bufs[3].at[d - 1], to_ring(d))
            for d in hops
        ]

    def first_half(bufs, src, ring, which):
        total = src[pl.ds(ring * 4 + which * 2, 2)].astype(F32)
        for d in range(3):
            total = total + bufs[0][d, pl.ds(which * 2, 2)].astype(F32)
        return total

    def sum_on_ring(bufs, src, ring, pair, to_pair, a_ring):
        arrive(a_ring)
        bufs[4][...] = first_half(bufs, src, ring, 1 - pair).astype(BF16)
        return push(bufs[4], bufs[5], to_pair)

    def sum_finish(bufs, src, ring, pair, b_ring, a_pair):
        arrive(b_ring)
        second = bufs[2][pl.ds(ring * 2, 2)].astype(F32)
        for d in range(3):
            second = second + bufs[3][d].astype(F32)
        a_pair.wait_recv()
        first = first_half(bufs, src, ring, pair) + bufs[5][...].astype(F32)
        return first[0], first[1], second[0], second[1]

    def tile_pass(c, forward, first, stop, acc):
        line = 0 if forward else 1
        panels = (H if forward else G)[c]

        def body(t, acc):
            for u in range(UNROLL):
                k = t * UNROLL + u
                entry = table[line, k]
                block = a_v[entry >> 7]
                panel = panels[(entry >> 1) & 63]
                if forward:
                    term = jnp.dot(block, panel, preferred_element_type=F32)
                else:
                    term = jnp.dot(panel, block, preferred_element_type=F32)
                acc = acc * (entry & 1).astype(F32) + term
                s_v[k] = acc.astype(BF16)
            return acc

        return lax.fori_loop(first // UNROLL, stop // UNROLL, body, acc)

    def collect(dst, line, count):
        def body(q, carry):
            for u in range(8):
                dst[q * 8 + u] = s_v[table[line, q * 8 + u]]
            return carry

        lax.fori_loop(0, count // 8, body, 0)

    zero = jnp.zeros((BLOCK, LANES), F32)

    def core_send(c):
        return push(R[c].at[pl.ds((1 - core) * 32, 32)], CX[c], at(core=1 - core))

    def core_add(c, copy):
        copy.wait_recv()

        def body(q, carry):
            for u in range(4):
                b = q * 4 + u
                T[c][b] = (R[c][core * 32 + b].astype(F32) + CX[c][b].astype(F32)).astype(BF16)
            return carry

        lax.fori_loop(0, 8, body, 0)

    def activate(c, blocks):
        lanes = slice(c * LANES, (c + 1) * LANES)
        held = []
        for b in range(4):
            nodes = slice(b * BLOCK, (b + 1) * BLOCK)
            act, slope = silu_parts(blocks[b])
            cot = cot_ref[nodes, lanes].astype(F32)
            grad = cot * rg_v[nodes, lanes] * slope
            G[c][col_slot(z, xh) + b] = grad.T.astype(BF16)
            held.append(act)
        return held

    def after_activate(c, held):
        lanes = slice(c * LANES, (c + 1) * LANES)
        act = jnp.concatenate(held, axis=0)
        lo_ref[:, lanes] = (act * rg_v[:, lanes]).astype(BF16)
        terms = jnp.dot(
            mt_v[...], cot_ref[:, lanes].astype(F32) * act,
            precision=lax.Precision.HIGHEST, preferred_element_type=F32,
        )
        for i in range(8):
            WP[c][i, 32:40] = terms[i * 8:(i + 1) * 8]

    to_core = at(core=1 - core)

    def share(c, ring, pair, first, count):
        got = G[c].at[pl.ds(col_slot(ring, pair) + first, count)]
        return push(got, got, to_core)

    def grad_send(c):
        pair_copy = gather_pair(G[c], col_slot, z, xh, col_pair)
        ring_copies = gather_ring(G[c], col_slot, z, xh, col_ring)
        return pair_copy, ring_copies, [share(c, z, xh, 0, 4)]

    def grad_on_pair(c, state):
        pair_copy, ring_copies, cores = state
        ring_a = gather_on_pair(G[c], col_slot, z, xh, col_ring, pair_copy)
        cores.append(share(c, z, 1 - xh, 0, 4))
        return ring_a, ring_copies, cores

    def grad_on_ring(c, state):
        ring_a, ring_copies, cores = state
        pair_b = gather_on_ring(G[c], col_slot, z, xh, col_pair, ring_copies)
        for d in hops:
            cores.append(share(c, (z + 4 - d) % 4, xh, 0, 4))
        return ring_a, pair_b, cores

    def grad_finish(c, state):
        ring_a, pair_b, cores = state
        for d, copy in zip(hops, ring_a):
            copy.wait_recv()
            cores.append(share(c, (z + 4 - d) % 4, 1 - xh, 0, 2))
        for d, copy in zip(hops, pair_b):
            copy.wait_recv()
            cores.append(share(c, (z + 4 - d) % 4, 1 - xh, 2, 2))
        arrive(cores)

    def finish_hidden(c, blocks):
        lanes = slice(c * LANES, (c + 1) * LANES)
        for b in range(4):
            hg_v[b * BLOCK:(b + 1) * BLOCK, lanes] = blocks[b].T.astype(BF16)
        part = jnp.dot(xt_v[...], hg_v[:, lanes], preferred_element_type=F32)
        for i in range(8):
            WP[c][i, 0:32] = part[i * 32:(i + 1) * 32]
        return [
            push(WP[c].at[(row + d) % 8], WR[c].at[d - 1], ((row + d) % 8, col))
            for d in range(1, 8)
        ]

    def weight_cols(c, copies):
        arrive(copies)
        total = WP[c][row]
        for d in range(7):
            total = total + WR[c][d]
        WS[c][...] = total
        return [
            push(WS[c], WC[c].at[d - 1], (row, (col + d) % 16)) for d in range(1, 16)
        ]

    def weight_rows(c, copies):
        arrive(copies)
        WC[c][15] = WS[c][...]
        total = jnp.zeros((48, LANES), F32)
        for j in range(16):
            total = total + WC[c][(col + 15 - j) % 16]
        WF[c][row, 0:32] = total[0:32] / 256.0
        WF[c][row, 32:48] = total[32:48]
        mine = WF[c].at[row]
        return [push(mine, mine, ((row + d) % 8, col)) for d in range(1, 8)]

    def weight_out(c, copies):
        arrive(copies)
        lanes = slice(c * LANES, (c + 1) * LANES)
        for i in range(8):
            wg_ref[i * 32:(i + 1) * 32, lanes] = WF[c][i, 0:32]
            gg_ref[i * 8:(i + 1) * 8, lanes] = WF[c][i, 32:40] / jnp.sqrt(WF[c][i, 40:48])

    gp0 = gather_pair(H[0], row_slot, y, xl, row_pair)
    gr0 = gather_ring(H[0], row_slot, y, xl, row_ring)
    for load in loads:
        load.start()
    gp1 = gather_pair(H[1], row_slot, y, xl, row_pair)
    spot = lax.broadcasted_iota(jnp.int32, (1, LANES), 1)
    rows, cols = rows_ref[...], cols_ref[...]
    block = rows % 4
    row_place = (rows // 4 % 2) * 32 + (rows // 8) * 4 + block
    within = spot % 32
    second = within - 16
    ring_at = jnp.where(within < 16, within // 4, second // 2 % 4)
    pair_at = jnp.where(within < 16, within // 2 % 2, second // 8)
    block_at = jnp.where(within < 16, within % 2, 2 + second % 2)
    row_order = ((ring_at * 2 + pair_at) * 2 + spot // 32) * 4 + block_at
    col_order = (pair_at * 4 + ring_at) * 4 + block_at
    live = live_ref[0, 0]
    entries, last = order_slots(rows, cols, live, 64, row_order)
    table_v[0:1] = entries
    table_v[2:3, 0:LANES] = last
    entries, last = order_slots(cols, row_place, live, 32, col_order)
    table_v[1:2] = entries
    table_v[3:4, 0:LANES] = last
    to_table = pltpu.make_async_copy(table_v, table, t_sem)
    to_table.start()
    ga0 = gather_on_pair(H[0], row_slot, y, xl, row_ring, gp0)
    s_v[SLOTS] = jnp.zeros((BLOCK, LANES), BF16)
    gb0 = gather_on_ring(H[0], row_slot, y, xl, row_pair, gr0)
    ids = lax.broadcasted_iota(jnp.int32, (PARTS, 4 * BLOCK), 0)
    mt_v[...] = (part_ref[...] == ids).astype(F32)
    sizes = jnp.dot(mt_v[...], jnp.ones((4 * BLOCK, LANES), F32), preferred_element_type=F32)
    for c in range(CHUNKS):
        for i in range(8):
            WP[c][i, 40:48] = sizes[i * 8:(i + 1) * 8]
    to_table.wait()
    for load in loads:
        load.wait()
    arrive(ga0 + gb0)
    gr1 = gather_ring(H[1], row_slot, y, xl, row_ring)
    ga1 = gather_on_pair(H[1], row_slot, y, xl, row_ring, gp1)

    acc = tile_pass(0, True, 0, 256, zero)
    gb1 = gather_on_ring(H[1], row_slot, y, xl, row_pair, gr1)
    tile_pass(0, True, 256, SLOTS, acc)
    collect(R[0], 2, 64)
    cs0 = core_send(0)
    rg_v[...] = lax.dot_general(
        mt_v[...], pg_ref[...], (((0,), (0,)), ((), ())),
        precision=lax.Precision.HIGHEST, preferred_element_type=F32,
    )
    xt_v[...] = x_ref[...].astype(F32).T.astype(BF16)
    arrive(ga1 + gb1)
    acc = tile_pass(1, True, 0, 64, zero)
    core_add(0, cs0)
    bp0, ar0 = sum_start(COL[0], T[0], z, xh, col_ring, col_pair)
    acc = tile_pass(1, True, 64, 288, acc)
    br0 = sum_on_pair(COL[0], T[0], z, xh, col_ring, bp0)
    tile_pass(1, True, 288, SLOTS, acc)
    collect(R[1], 2, 64)
    cs1 = core_send(1)
    ap0 = sum_on_ring(COL[0], T[0], z, xh, col_pair, ar0)
    core_add(1, cs1)
    held0 = activate(0, sum_finish(COL[0], T[0], z, xh, br0, ap0))
    gs0 = grad_send(0)
    bp1, ar1 = sum_start(COL[1], T[1], z, xh, col_ring, col_pair)
    after_activate(0, held0)
    gs0 = grad_on_pair(0, gs0)
    gs0 = grad_on_ring(0, gs0)
    br1 = sum_on_pair(COL[1], T[1], z, xh, col_ring, bp1)
    ap1 = sum_on_ring(COL[1], T[1], z, xh, col_pair, ar1)
    grad_finish(0, gs0)
    acc = tile_pass(0, False, 0, 64, zero)
    held1 = activate(1, sum_finish(COL[1], T[1], z, xh, br1, ap1))
    gs1 = grad_send(1)
    after_activate(1, held1)
    acc = tile_pass(0, False, 64, 192, acc)
    gs1 = grad_on_pair(1, gs1)
    acc = tile_pass(0, False, 192, 320, acc)
    gs1 = grad_on_ring(1, gs1)
    tile_pass(0, False, 320, SLOTS, acc)
    collect(PP[0], 3, 32)
    bq0, aq0 = sum_start(ROW[0], PP[0], y, xl, row_ring, row_pair)
    grad_finish(1, gs1)
    acc = tile_pass(1, False, 0, 256, zero)
    dq0 = sum_on_pair(ROW[0], PP[0], y, xl, row_ring, bq0)
    acc = tile_pass(1, False, 256, SLOTS, acc)
    collect(PP[1], 3, 32)
    bq1, aq1 = sum_start(ROW[1], PP[1], y, xl, row_ring, row_pair)
    eq0 = sum_on_ring(ROW[0], PP[0], y, xl, row_pair, aq0)
    wr0_ = finish_hidden(0, sum_finish(ROW[0], PP[0], y, xl, dq0, eq0))
    dq1 = sum_on_pair(ROW[1], PP[1], y, xl, row_ring, bq1)
    wc0_ = weight_cols(0, wr0_)
    eq1 = sum_on_ring(ROW[1], PP[1], y, xl, row_pair, aq1)
    wr1_ = finish_hidden(1, sum_finish(ROW[1], PP[1], y, xl, dq1, eq1))
    fg_ref[...] = lax.dot_general(
        hg_v[...], w_ref[...], (((1,), (1,)), ((), ())), preferred_element_type=F32
    ).astype(BF16)
    wf0_ = weight_rows(0, wc0_)
    wc1_ = weight_cols(1, wr1_)
    weight_out(0, wf0_)
    wf1_ = weight_rows(1, wc1_)
    weight_out(1, wf1_)
    for copy in started:
        copy.wait_send()


def hand_over(*refs):
    half = len(refs) // 2
    for src, dst in zip(refs[:half], refs[half:]):
        dst[...] = src[...]


def per_device(
    features, weight, adjacency, block_rows, block_cols, live_blocks, part_gains, partition, cotangent
):
    nodes = features.shape[0]
    smem = pl.BlockSpec(memory_space=pltpu.SMEM)
    vmem = pl.BlockSpec(memory_space=pltpu.VMEM)
    hbm = pl.BlockSpec(memory_space=pl.ANY)

    def pair(shape, dtype=BF16):
        return [pltpu.VMEM(shape, dtype)] * 2

    tile = (BLOCK, LANES)
    sums = [
        *pair((3, 4) + tile), *pair((8,) + tile), *pair((8,) + tile),
        *pair((3, 2) + tile), *pair((2,) + tile), *pair((2,) + tile),
    ]
    copies = 160
    outs = (
        jax.ShapeDtypeStruct((nodes, WIDTH), BF16),
        jax.ShapeDtypeStruct((nodes, WIDTH), BF16),
        jax.ShapeDtypeStruct((WIDTH, WIDTH), F32),
        jax.ShapeDtypeStruct((PARTS, WIDTH), F32),
    )
    results = pl.pallas_call(
        kernel,
        out_shape=outs,
        in_specs=[vmem, vmem, smem, vmem, vmem, hbm, vmem, vmem, vmem],
        out_specs=(vmem,) * 4,
        scratch_shapes=[
            pltpu.VMEM((8, SLOTS), jnp.int32),
            pltpu.SMEM((8, SLOTS), jnp.int32),
            pltpu.VMEM((SLOTS,) + tile, BF16),
            pltpu.VMEM((SLOTS + 1,) + tile, BF16),
            *pair((32,) + tile), *pair((64,) + tile), *pair((32,) + tile), *pair((32,) + tile),
            *pair((64,) + tile), *pair((32,) + tile),
            *sums, *sums,
            *pair((8, 48, LANES), F32), *pair((7, 48, LANES), F32), *pair((48, LANES), F32),
            *pair((16, 48, LANES), F32), *pair((8, 48, LANES), F32),
            pltpu.VMEM((nodes, WIDTH), F32),
            pltpu.VMEM((PARTS, nodes), F32),
            pltpu.VMEM((WIDTH, nodes), BF16),
            pltpu.VMEM((nodes, WIDTH), BF16),
            pltpu.SemaphoreType.DMA((4,)),
            pltpu.SemaphoreType.DMA,
            pltpu.SemaphoreType.DMA((copies,)),
            pltpu.SemaphoreType.DMA((copies,)),
        ],
        compiler_params=pltpu.CompilerParams(
            collective_id=0, has_side_effects=True, vmem_limit_bytes=60 * 2**20
        ),
    )(
        block_rows.reshape(1, SLOTS), block_cols.reshape(1, SLOTS), live_blocks,
        features, weight, adjacency[0, 0], part_gains, partition.reshape(1, nodes), cotangent,
    )
    return pl.pallas_call(
        hand_over,
        out_shape=outs,
        in_specs=[vmem] * 4,
        out_specs=(vmem,) * 4,
    )(*results)


def solution(mesh):
    in_specs = (
        P(("row", "col"), None),
        P(),
        P("row", "col", None, None, None),
        P("row", "col", None),
        P("row", "col", None),
        P("row", "col"),
        P(),
        P(("row", "col")),
        P(("row", "col"), None),
    )
    out_specs = (P(("row", "col"), None), P(("row", "col"), None), P(), P())
    return jax.shard_map(
        per_device, mesh=mesh, in_specs=in_specs, out_specs=out_specs, check_vma=False
    )
```

time: 166 us -> 135 us (0.81)
  Pallas kernels: 151 us -> 134 us
  other arithmetic: 6.57 us -> 0 us
  local copies, waits for them, and re-layouts: 6.48 us -> 0 us
    pallas_call x1 -> x2, Pallas kernels: 151 us -> 134 us  [the longest x1 132 us: per_device(): pl.pallas_call(kernel, out_shape=outs, in_specs=[vmem, vmem, smem, vmem,...]
    unnamed x4 -> x0, local copies, waits for them, and re-layouts: 6.48 us -> none
    select_n x4 -> x0, other arithmetic: 2.29 us -> none  [the longest x2 1.18 us: order_slots(): sorted_key = ranked // 128 % 128]
where the time goes in v2:
time: 135 us
  Pallas kernels  134 us (99%)
    pallas_call x1, Pallas kernels, per_device(): pl.pallas_call(kernel, out_shape=outs, in_specs=[vmem, vmem, smem, vmem,...  132 us

profile of v2, /device:TPU:1, one launch (start us, length us, event | category | flops | bytes accessed | tf_op | source)
XLA Modules:
  0.0 134.9 jit_solution(6388816321732783865)
XLA Ops:
  1.3 131.6 %shard_map.120 = (bf16[512,256]{1,0:T(8,128)(2,1)}, bf16[512,256]{1,0:T(8,128)(2,1)}, f32[256,256]{1,0:T(8,128)}, f32[64,256]{1,0:T(8,128)}) custom-call(s32[1,384]{1,0:T(1,128)} %bitcast.6, s32[1,384]{1,0:T(1,128)} %bitcast.7, s32[1,1]{1,0:T(1,128)S(6)} %copy.13.live_ref, bf16[512,256]{1,0:T(8,128)(2,1)} %x_ref.1, bf16[256,256]{1,0:T(8,128)(2,1)} %w_ref.1, ...), custom_call_target="tpu_custom_call" | custom-call | tf_op jit(solution)/shard_map/pallas_call | solution.py:457
  132.9 2.0 %shard_map.121 = (bf16[512,256]{1,0:T(8,128)(2,1)}, bf16[512,256]{1,0:T(8,128)(2,1)}, f32[256,256]{1,0:T(8,128)}, f32[64,256]{1,0:T(8,128)}) custom-call(bf16[512,256]{1,0:T(8,128)(2,1)} %get-tuple-element.8.refs_0_, bf16[512,256]{1,0:T(8,128)(2,1)} %get-tuple-element.9.refs_1_, f32[256,256]{1,0:T(8,128)} %get-tuple-element.10.refs_2_, ...), custom_call_target="tpu_custom_call" | custom-call | tf_op jit(solution)/shard_map/pallas_call | solution.py:488

commit v3 on v2

--- a/solution.py
+++ b/solution.py
@@ -57,7 +57,7 @@
     ca0, ca1, cp0, cp1, cm0, cm1, cb0, cb1, cs0_, cs1_, cl0, cl1,
     ra0, ra1, rp0, rp1, rm0, rm1, rb0, rb1, rs0_, rs1_, rl0, rl1,
     wp0, wp1, wr0, wr1, ws0, ws1, wc0, wc1, wf0, wf1,
-    rg_v, mt_v, xt_v, hg_v,
+    rg_v, mt_v, xg_v, hg_v,
     a_sem, t_sem, send, recv,
 ):
     row = lax.axis_index("row")
@@ -104,59 +104,58 @@
     for d in range(1, 16):
         pl.semaphore_signal(barrier, inc=1, device_id=(row, (col + d) % 16), device_id_type=MESH)
 
-    own_h = pl.ds(row * 4, 4)
     for c in range(CHUNKS):
         hidden = jnp.dot(x_ref[...], w_ref[:, c * LANES:(c + 1) * LANES], preferred_element_type=F32)
-        H[c][own_h] = hidden.astype(BF16).reshape(4, BLOCK, LANES)
+        hidden = hidden.astype(BF16).reshape(4, BLOCK, LANES)
+        H[c][pl.ds(y * 8 + xl * 2, 2)] = hidden[0:2]
+        H[c][pl.ds(y * 8 + 4 + xl * 2, 2)] = hidden[2:4]
     pl.semaphore_wait(barrier, 22)
 
     row_ring, row_pair = (lambda d: at(y=(y + d) % 4)), at(xl=1 - xl)
     col_ring, col_pair = (lambda d: at(z=(z + d) % 4)), at(xh=1 - xh)
     hops = (1, 3, 2)
 
-    def gather_pair(buf, slot_of, ring, pair, to_pair):
-        mine = buf.at[pl.ds(slot_of(ring, pair), 4)]
-        return push(mine, mine, to_pair)
-
-    def gather_ring(buf, slot_of, ring, pair, to_ring):
-        mine = buf.at[pl.ds(slot_of(ring, pair), 4)]
-        return [push(mine, mine, to_ring(d)) for d in hops]
-
-    def gather_on_pair(buf, slot_of, ring, pair, to_ring, pair_copy):
-        pair_copy.wait_recv()
-        other = buf.at[pl.ds(slot_of(ring, 1 - pair), 2)]
-        return [push(other, other, to_ring(d)) for d in hops]
-
-    def gather_on_ring(buf, slot_of, ring, pair, to_pair, ring_copies):
+    def gather_start(buf, base, ring, pair, to_ring, to_pair):
+        first = buf.at[pl.ds(base + ring * 8 + pair * 2, 2)]
+        second = buf.at[pl.ds(base + ring * 8 + 4 + pair * 2, 2)]
+        a_pair = push(first, first, to_pair)
+        b_ring = [push(second, second, to_ring(d)) for d in hops]
+        return a_pair, b_ring, push(second, second, to_pair)
+
+    def gather_on_pair(buf, base, ring, to_ring, a_pair):
+        a_pair.wait_recv()
+        both = buf.at[pl.ds(base + ring * 8, 4)]
+        return [push(both, both, to_ring(d)) for d in hops]
+
+    def gather_on_ring(buf, base, ring, pair, to_pair, b_ring):
         out = []
-        for d, copy in zip(hops, ring_copies):
+        for d, copy in zip(hops, b_ring):
             copy.wait_recv()
-            got = buf.at[pl.ds(slot_of((ring + 4 - d) % 4, pair) + 2, 2)]
+            got = buf.at[pl.ds(base + (ring + 4 - d) % 4 * 8 + 4 + pair * 2, 2)]
             out.append(push(got, got, to_pair))
         return out
 
-    def row_slot(ring, pair):
-        return (pair * 4 + ring) * 4
-
-    def col_slot(ring, pair):
-        return core * 32 + (ring * 2 + pair) * 4
-
     def sum_start(bufs, src, ring, pair, to_ring, to_pair):
-        b_pair = push(src.at[pl.ds(16 + (1 - pair) * 8, 8)], bufs[1], to_pair)
+        b_pair = []
+        for d in (2, 1, 3, 0):
+            spot = (ring + d) % 4 * 2
+            b_pair.append(
+                push(src.at[pl.ds(16 + (1 - pair) * 8 + spot, 2)], bufs[1].at[pl.ds(spot, 2)], to_pair)
+            )
         a_ring = [
             push(src.at[pl.ds(((ring + d) % 4) * 4, 4)], bufs[0].at[d - 1], to_ring(d)) for d in hops
         ]
         return b_pair, a_ring
 
     def sum_on_pair(bufs, src, ring, pair, to_ring, b_pair):
-        b_pair.wait_recv()
-        bufs[2][...] = (
-            src[pl.ds(16 + pair * 8, 8)].astype(F32) + bufs[1][...].astype(F32)
-        ).astype(BF16)
-        return [
-            push(bufs[2].at[pl.ds(((ring + d) % 4) * 2, 2)], bufs[3].at[d - 1], to_ring(d))
-            for d in hops
-        ]
+        out = []
+        for d, copy in zip((2, 1, 3), b_pair):
+            copy.wait_recv()
+            spot = pl.ds((ring + d) % 4 * 2, 2)
+            mine = src[pl.ds(16 + pair * 8 + (ring + d) % 4 * 2, 2)]
+            bufs[2][spot] = (mine.astype(F32) + bufs[1][spot].astype(F32)).astype(BF16)
+            out.append(push(bufs[2].at[spot], bufs[3].at[d - 1], to_ring(d)))
+        return out, b_pair[3]
 
     def first_half(bufs, src, ring, which):
         total = src[pl.ds(ring * 4 + which * 2, 2)].astype(F32)
@@ -169,9 +168,12 @@
         bufs[4][...] = first_half(bufs, src, ring, 1 - pair).astype(BF16)
         return push(bufs[4], bufs[5], to_pair)
 
-    def sum_finish(bufs, src, ring, pair, b_ring, a_pair):
+    def sum_finish(bufs, src, ring, pair, on_pair, a_pair):
+        b_ring, b_own = on_pair
+        b_own.wait_recv()
         arrive(b_ring)
-        second = bufs[2][pl.ds(ring * 2, 2)].astype(F32)
+        second = src[pl.ds(16 + pair * 8 + ring * 2, 2)].astype(F32)
+        second = second + bufs[1][pl.ds(ring * 2, 2)].astype(F32)
         for d in range(3):
             second = second + bufs[3][d].astype(F32)
         a_pair.wait_recv()
@@ -230,7 +232,7 @@
             act, slope = silu_parts(blocks[b])
             cot = cot_ref[nodes, lanes].astype(F32)
             grad = cot * rg_v[nodes, lanes] * slope
-            G[c][col_slot(z, xh) + b] = grad.T.astype(BF16)
+            G[c][core * 32 + z * 8 + b // 2 * 4 + xh * 2 + b % 2] = grad.T.astype(BF16)
             held.append(act)
         return held
 
@@ -247,43 +249,45 @@
 
     to_core = at(core=1 - core)
 
-    def share(c, ring, pair, first, count):
-        got = G[c].at[pl.ds(col_slot(ring, pair) + first, count)]
+    def share(c, first, count):
+        got = G[c].at[pl.ds(core * 32 + first, count)]
         return push(got, got, to_core)
 
-    def grad_send(c):
-        pair_copy = gather_pair(G[c], col_slot, z, xh, col_pair)
-        ring_copies = gather_ring(G[c], col_slot, z, xh, col_ring)
-        return pair_copy, ring_copies, [share(c, z, xh, 0, 4)]
+    def grad_start(c):
+        return gather_start(G[c], core * 32, z, xh, col_ring, col_pair)
 
     def grad_on_pair(c, state):
-        pair_copy, ring_copies, cores = state
-        ring_a = gather_on_pair(G[c], col_slot, z, xh, col_ring, pair_copy)
-        cores.append(share(c, z, 1 - xh, 0, 4))
-        return ring_a, ring_copies, cores
+        a_pair, b_ring, b_pair = state
+        return gather_on_pair(G[c], core * 32, z, col_ring, a_pair), b_ring, b_pair
 
     def grad_on_ring(c, state):
-        ring_a, ring_copies, cores = state
-        pair_b = gather_on_ring(G[c], col_slot, z, xh, col_pair, ring_copies)
-        for d in hops:
-            cores.append(share(c, (z + 4 - d) % 4, xh, 0, 4))
-        return ring_a, pair_b, cores
+        a_ring, b_ring, b_pair = state
+        b_other = gather_on_ring(G[c], core * 32, z, xh, col_pair, b_ring)
+        b_pair.wait_recv()
+        return a_ring, b_other, [share(c, z * 8, 8)]
 
     def grad_finish(c, state):
-        ring_a, pair_b, cores = state
-        for d, copy in zip(hops, ring_a):
-            copy.wait_recv()
-            cores.append(share(c, (z + 4 - d) % 4, 1 - xh, 0, 2))
-        for d, copy in zip(hops, pair_b):
-            copy.wait_recv()
-            cores.append(share(c, (z + 4 - d) % 4, 1 - xh, 2, 2))
+        a_ring, b_other, cores = state
+        for half, copies in ((0, a_ring), (4, b_other)):
+            for d, copy in zip(hops, copies):
+                copy.wait_recv()
+                cores.append(share(c, (z + 4 - d) % 4 * 8 + half, 4))
         arrive(cores)
 
     def finish_hidden(c, blocks):
         lanes = slice(c * LANES, (c + 1) * LANES)
         for b in range(4):
             hg_v[b * BLOCK:(b + 1) * BLOCK, lanes] = blocks[b].T.astype(BF16)
-        part = jnp.dot(xt_v[...], hg_v[:, lanes], preferred_element_type=F32)
+
+    def weight_part(c):
+        part = jnp.zeros((LANES, WIDTH), F32)
+        for i in range(8):
+            for b in range(4):
+                pair, ring = i // 4, i % 4
+                spot = ring * 4 + pair * 2 + b if b < 2 else 16 + pair * 8 + ring * 2 + b - 2
+                nodes = slice((i * 4 + b) * BLOCK, (i * 4 + b + 1) * BLOCK)
+                part = part + jnp.dot(PP[c][spot], xg_v[nodes], preferred_element_type=F32)
+        part = part.T
         for i in range(8):
             WP[c][i, 0:32] = part[i * 32:(i + 1) * 32]
         return [
@@ -319,15 +323,17 @@
             wg_ref[i * 32:(i + 1) * 32, lanes] = WF[c][i, 0:32]
             gg_ref[i * 8:(i + 1) * 8, lanes] = WF[c][i, 32:40] / jnp.sqrt(WF[c][i, 40:48])
 
-    gp0 = gather_pair(H[0], row_slot, y, xl, row_pair)
-    gr0 = gather_ring(H[0], row_slot, y, xl, row_ring)
+    gs0 = gather_start(H[0], 0, y, xl, row_ring, row_pair)
     for load in loads:
         load.start()
-    gp1 = gather_pair(H[1], row_slot, y, xl, row_pair)
     spot = lax.broadcasted_iota(jnp.int32, (1, LANES), 1)
     rows, cols = rows_ref[...], cols_ref[...]
     block = rows % 4
-    row_place = (rows // 4 % 2) * 32 + (rows // 8) * 4 + block
+    row_place = (
+        rows // 4 % 2 * 32 + rows // 16 * 8 + block // 2 * 4 + rows // 8 % 2 * 2 + block % 2
+    )
+    block = cols % 4
+    col_place = cols // 4 % 4 * 8 + block // 2 * 4 + cols // 16 * 2 + block % 2
     within = spot % 32
     second = within - 16
     ring_at = jnp.where(within < 16, within // 4, second // 2 % 4)
@@ -336,7 +342,7 @@
     row_order = ((ring_at * 2 + pair_at) * 2 + spot // 32) * 4 + block_at
     col_order = (pair_at * 4 + ring_at) * 4 + block_at
     live = live_ref[0, 0]
-    entries, last = order_slots(rows, cols, live, 64, row_order)
+    entries, last = order_slots(rows, col_place, live, 64, row_order)
     table_v[0:1] = entries
     table_v[2:3, 0:LANES] = last
     entries, last = order_slots(cols, row_place, live, 32, col_order)
@@ -344,82 +350,89 @@
     table_v[3:4, 0:LANES] = last
     to_table = pltpu.make_async_copy(table_v, table, t_sem)
     to_table.start()
-    ga0 = gather_on_pair(H[0], row_slot, y, xl, row_ring, gp0)
-    s_v[SLOTS] = jnp.zeros((BLOCK, LANES), BF16)
-    gb0 = gather_on_ring(H[0], row_slot, y, xl, row_pair, gr0)
+    ga0 = gather_on_pair(H[0], 0, y, row_ring, gs0[0])
     ids = lax.broadcasted_iota(jnp.int32, (PARTS, 4 * BLOCK), 0)
     mt_v[...] = (part_ref[...] == ids).astype(F32)
+    xg_v[pl.ds(row * 512, 512)] = x_ref[...]
+    s_v[SLOTS] = jnp.zeros((BLOCK, LANES), BF16)
+    gb0 = gather_on_ring(H[0], 0, y, xl, row_pair, gs0[1])
+    to_table.wait()
+    for load in loads:
+        load.wait()
+    arrive(ga0 + gb0 + [gs0[2]])
+    gs1 = gather_start(H[1], 0, y, xl, row_ring, row_pair)
+
+    acc = tile_pass(0, True, 0, 160, zero)
+    ga1 = gather_on_pair(H[1], 0, y, row_ring, gs1[0])
+    acc = tile_pass(0, True, 160, 256, acc)
+    gb1 = gather_on_ring(H[1], 0, y, xl, row_pair, gs1[1])
+    tile_pass(0, True, 256, SLOTS, acc)
+    collect(R[0], 2, 64)
+    cs0 = core_send(0)
     sizes = jnp.dot(mt_v[...], jnp.ones((4 * BLOCK, LANES), F32), preferred_element_type=F32)
     for c in range(CHUNKS):
         for i in range(8):
             WP[c][i, 40:48] = sizes[i * 8:(i + 1) * 8]
-    to_table.wait()
-    for load in loads:
-        load.wait()
-    arrive(ga0 + gb0)
-    gr1 = gather_ring(H[1], row_slot, y, xl, row_ring)
-    ga1 = gather_on_pair(H[1], row_slot, y, xl, row_ring, gp1)
-
-    acc = tile_pass(0, True, 0, 256, zero)
-    gb1 = gather_on_ring(H[1], row_slot, y, xl, row_pair, gr1)
-    tile_pass(0, True, 256, SLOTS, acc)
-    collect(R[0], 2, 64)
-    cs0 = core_send(0)
     rg_v[...] = lax.dot_general(
         mt_v[...], pg_ref[...], (((0,), (0,)), ((), ())),
         precision=lax.Precision.HIGHEST, preferred_element_type=F32,
     )
-    xt_v[...] = x_ref[...].astype(F32).T.astype(BF16)
-    arrive(ga1 + gb1)
-    acc = tile_pass(1, True, 0, 64, zero)
     core_add(0, cs0)
     bp0, ar0 = sum_start(COL[0], T[0], z, xh, col_ring, col_pair)
-    acc = tile_pass(1, True, 64, 288, acc)
+    arrive(ga1 + gb1 + [gs1[2]])
+    own_x = xg_v.at[pl.ds(row * 512, 512)]
+    px = push(own_x, own_x, row_pair)
+    rx = [push(own_x, own_x, row_ring(d)) for d in hops]
+    acc = tile_pass(1, True, 0, 128, zero)
     br0 = sum_on_pair(COL[0], T[0], z, xh, col_ring, bp0)
-    tile_pass(1, True, 288, SLOTS, acc)
+    tile_pass(1, True, 128, SLOTS, acc)
     collect(R[1], 2, 64)
     cs1 = core_send(1)
     ap0 = sum_on_ring(COL[0], T[0], z, xh, col_pair, ar0)
     core_add(1, cs1)
+    bp1, ar1 = sum_start(COL[1], T[1], z, xh, col_ring, col_pair)
     held0 = activate(0, sum_finish(COL[0], T[0], z, xh, br0, ap0))
-    gs0 = grad_send(0)
-    bp1, ar1 = sum_start(COL[1], T[1], z, xh, col_ring, col_pair)
+    gg0 = grad_start(0)
+    px.wait_recv()
+    other_x = xg_v.at[pl.ds(((1 - xl) * 4 + y) * 512, 512)]
+    rx += [push(other_x, other_x, row_ring(d)) for d in hops]
+    br1 = sum_on_pair(COL[1], T[1], z, xh, col_ring, bp1)
+    gg0 = grad_on_pair(0, gg0)
     after_activate(0, held0)
-    gs0 = grad_on_pair(0, gs0)
-    gs0 = grad_on_ring(0, gs0)
-    br1 = sum_on_pair(COL[1], T[1], z, xh, col_ring, bp1)
+    gg0 = grad_on_ring(0, gg0)
     ap1 = sum_on_ring(COL[1], T[1], z, xh, col_pair, ar1)
-    grad_finish(0, gs0)
-    acc = tile_pass(0, False, 0, 64, zero)
     held1 = activate(1, sum_finish(COL[1], T[1], z, xh, br1, ap1))
-    gs1 = grad_send(1)
-    after_activate(1, held1)
-    acc = tile_pass(0, False, 64, 192, acc)
-    gs1 = grad_on_pair(1, gs1)
-    acc = tile_pass(0, False, 192, 320, acc)
-    gs1 = grad_on_ring(1, gs1)
-    tile_pass(0, False, 320, SLOTS, acc)
+    gg1 = grad_start(1)
+    grad_finish(0, gg0)
+    gg1 = grad_on_pair(1, gg1)
+    acc = tile_pass(0, False, 0, 96, zero)
+    gg1 = grad_on_ring(1, gg1)
+    tile_pass(0, False, 96, SLOTS, acc)
     collect(PP[0], 3, 32)
     bq0, aq0 = sum_start(ROW[0], PP[0], y, xl, row_ring, row_pair)
-    grad_finish(1, gs1)
-    acc = tile_pass(1, False, 0, 256, zero)
+    after_activate(1, held1)
+    arrive(rx)
+    grad_finish(1, gg1)
+    acc = tile_pass(1, False, 0, 128, zero)
     dq0 = sum_on_pair(ROW[0], PP[0], y, xl, row_ring, bq0)
-    acc = tile_pass(1, False, 256, SLOTS, acc)
+    acc = tile_pass(1, False, 128, SLOTS, acc)
     collect(PP[1], 3, 32)
     bq1, aq1 = sum_start(ROW[1], PP[1], y, xl, row_ring, row_pair)
     eq0 = sum_on_ring(ROW[0], PP[0], y, xl, row_pair, aq0)
-    wr0_ = finish_hidden(0, sum_finish(ROW[0], PP[0], y, xl, dq0, eq0))
+    wr0_ = weight_part(0)
+    wr1_ = weight_part(1)
+    finish_hidden(0, sum_finish(ROW[0], PP[0], y, xl, dq0, eq0))
     dq1 = sum_on_pair(ROW[1], PP[1], y, xl, row_ring, bq1)
     wc0_ = weight_cols(0, wr0_)
+    wc1_ = weight_cols(1, wr1_)
     eq1 = sum_on_ring(ROW[1], PP[1], y, xl, row_pair, aq1)
-    wr1_ = finish_hidden(1, sum_finish(ROW[1], PP[1], y, xl, dq1, eq1))
+    wf0_ = weight_rows(0, wc0_)
+    wf1_ = weight_rows(1, wc1_)
+    finish_hidden(1, sum_finish(ROW[1], PP[1], y, xl, dq1, eq1))
     fg_ref[...] = lax.dot_general(
         hg_v[...], w_ref[...], (((1,), (1,)), ((), ())), preferred_element_type=F32
     ).astype(BF16)
-    wf0_ = weight_rows(0, wc0_)
-    wc1_ = weight_cols(1, wr1_)
     weight_out(0, wf0_)
-    wf1_ = weight_rows(1, wc1_)
     weight_out(1, wf1_)
     for copy in started:
         copy.wait_send()
@@ -447,7 +460,7 @@
         *pair((3, 4) + tile), *pair((8,) + tile), *pair((8,) + tile),
         *pair((3, 2) + tile), *pair((2,) + tile), *pair((2,) + tile),
     ]
-    copies = 160
+    copies = 176
     outs = (
         jax.ShapeDtypeStruct((nodes, WIDTH), BF16),
         jax.ShapeDtypeStruct((nodes, WIDTH), BF16),
@@ -471,7 +484,7 @@
             *pair((16, 48, LANES), F32), *pair((8, 48, LANES), F32),
             pltpu.VMEM((nodes, WIDTH), F32),
             pltpu.VMEM((PARTS, nodes), F32),
-            pltpu.VMEM((WIDTH, nodes), BF16),
+            pltpu.VMEM((8 * nodes, WIDTH), BF16),
             pltpu.VMEM((nodes, WIDTH), BF16),
             pltpu.SemaphoreType.DMA((4,)),
             pltpu.SemaphoreType.DMA,

time: 135 us -> 118 us (0.87)
  Pallas kernels: 134 us -> 117 us
    pallas_call x1, Pallas kernels: 132 us -> 115 us  [per_device(): pl.pallas_call(kernel, out_shape=outs, in_specs=[vmem, vmem, smem, vmem,...]
where the time goes in v3:
time: 118 us
  Pallas kernels  117 us (99%)
  between operations  1.29 us (1%)
    pallas_call x1, Pallas kernels, per_device(): pl.pallas_call(kernel, out_shape=outs, in_specs=[vmem, vmem, smem, vmem,...  115 us

profile of v3, /device:TPU:1, one launch (start us, length us, event | category | flops | bytes accessed | tf_op | source)
XLA Modules:
  0.0 117.8 jit_solution(3793950060884517695)
XLA Ops:
  1.3 114.5 %shard_map.120 = (bf16[512,256]{1,0:T(8,128)(2,1)}, bf16[512,256]{1,0:T(8,128)(2,1)}, f32[256,256]{1,0:T(8,128)}, f32[64,256]{1,0:T(8,128)}) custom-call(s32[1,384]{1,0:T(1,128)} %bitcast.6, s32[1,384]{1,0:T(1,128)} %bitcast.7, s32[1,1]{1,0:T(1,128)S(6)} %copy.13.live_ref, bf16[512,256]{1,0:T(8,128)(2,1)} %x_ref.1, bf16[256,256]{1,0:T(8,128)(2,1)} %w_ref.1, ...), custom_call_target="tpu_custom_call" | custom-call | tf_op jit(solution)/shard_map/pallas_call | solution.py:470
  115.8 2.0 %shard_map.121 = (bf16[512,256]{1,0:T(8,128)(2,1)}, bf16[512,256]{1,0:T(8,128)(2,1)}, f32[256,256]{1,0:T(8,128)}, f32[64,256]{1,0:T(8,128)}) custom-call(bf16[512,256]{1,0:T(8,128)(2,1)} %get-tuple-element.8.refs_0_, bf16[512,256]{1,0:T(8,128)(2,1)} %get-tuple-element.9.refs_1_, f32[256,256]{1,0:T(8,128)} %get-tuple-element.10.refs_2_, ...), custom_call_target="tpu_custom_call" | custom-call | tf_op jit(solution)/shard_map/pallas_call | solution.py:501

commit v4 on v3

--- a/solution.py
+++ b/solution.py
@@ -56,7 +56,7 @@
     table_v, table, a_v, s_v, h0, h1, r0, r1, cx0, cx1, t0, t1, g0, g1, p0, p1,
     ca0, ca1, cp0, cp1, cm0, cm1, cb0, cb1, cs0_, cs1_, cl0, cl1,
     ra0, ra1, rp0, rp1, rm0, rm1, rb0, rb1, rs0_, rs1_, rl0, rl1,
-    wp0, wp1, wr0, wr1, ws0, ws1, wc0, wc1, wf0, wf1,
+    wp, wr, ws, wk, wc, wf,
     rg_v, mt_v, xg_v, hg_v,
     a_sem, t_sem, send, recv,
 ):
@@ -71,7 +71,6 @@
     H, R, CX, T, G, PP = (h0, h1), (r0, r1), (cx0, cx1), (t0, t1), (g0, g1), (p0, p1)
     COL = ((ca0, cp0, cm0, cb0, cs0_, cl0), (ca1, cp1, cm1, cb1, cs1_, cl1))
     ROW = ((ra0, rp0, rm0, rb0, rs0_, rl0), (ra1, rp1, rm1, rb1, rs1_, rl1))
-    WP, WR, WS, WC, WF = (wp0, wp1), (wr0, wr1), (ws0, ws1), (wc0, wc1), (wf0, wf1)
 
     started = []
 
@@ -99,17 +98,17 @@
     ]
 
     barrier = pltpu.get_barrier_semaphore()
-    for d in range(1, 8):
-        pl.semaphore_signal(barrier, inc=1, device_id=((row + d) % 8, col), device_id_type=MESH)
-    for d in range(1, 16):
-        pl.semaphore_signal(barrier, inc=1, device_id=(row, (col + d) % 16), device_id_type=MESH)
+    near = [at(xl=1 - xl), at(xh=1 - xh), at(core=1 - core)]
+    near += [at(y=(y + d) % 4) for d in (1, 3, 2)] + [at(z=(z + d) % 4) for d in (1, 3, 2)]
+    for device in near:
+        pl.semaphore_signal(barrier, inc=1, device_id=device, device_id_type=MESH)
 
     for c in range(CHUNKS):
         hidden = jnp.dot(x_ref[...], w_ref[:, c * LANES:(c + 1) * LANES], preferred_element_type=F32)
         hidden = hidden.astype(BF16).reshape(4, BLOCK, LANES)
         H[c][pl.ds(y * 8 + xl * 2, 2)] = hidden[0:2]
         H[c][pl.ds(y * 8 + 4 + xl * 2, 2)] = hidden[2:4]
-    pl.semaphore_wait(barrier, 22)
+    pl.semaphore_wait(barrier, 9)
 
     row_ring, row_pair = (lambda d: at(y=(y + d) % 4)), at(xl=1 - xl)
     col_ring, col_pair = (lambda d: at(z=(z + d) % 4)), at(xh=1 - xh)
@@ -135,17 +134,28 @@
             out.append(push(got, got, to_pair))
         return out
 
-    def sum_start(bufs, src, ring, pair, to_ring, to_pair):
+    def gather_second(buf, base, ring, pair, to_ring, b_pair):
+        b_pair.wait_recv()
+        other = buf.at[pl.ds(base + ring * 8 + 4 + (1 - pair) * 2, 2)]
+        return [push(other, other, to_ring(d)) for d in hops]
+
+    def sum_start_pair(bufs, src, ring, pair, to_pair):
         b_pair = []
         for d in (2, 1, 3, 0):
             spot = (ring + d) % 4 * 2
             b_pair.append(
                 push(src.at[pl.ds(16 + (1 - pair) * 8 + spot, 2)], bufs[1].at[pl.ds(spot, 2)], to_pair)
             )
-        a_ring = [
+        return b_pair
+
+    def sum_start_ring(bufs, src, ring, to_ring):
+        return [
             push(src.at[pl.ds(((ring + d) % 4) * 4, 4)], bufs[0].at[d - 1], to_ring(d)) for d in hops
         ]
-        return b_pair, a_ring
+
+    def row_start(c):
+        b_pair = sum_start_pair(ROW[c], PP[c], y, xl, row_pair)
+        return b_pair, sum_start_ring(ROW[c], PP[c], y, row_ring)
 
     def sum_on_pair(bufs, src, ring, pair, to_ring, b_pair):
         out = []
@@ -200,29 +210,39 @@
 
         return lax.fori_loop(first // UNROLL, stop // UNROLL, body, acc)
 
-    def collect(dst, line, count):
+    def collect(dst, line, first):
         def body(q, carry):
             for u in range(8):
-                dst[q * 8 + u] = s_v[table[line, q * 8 + u]]
+                b = first + q * 8 + u
+                dst[b] = s_v[table[line, b]]
             return carry
 
-        lax.fori_loop(0, count // 8, body, 0)
+        lax.fori_loop(0, 4, body, 0)
 
     zero = jnp.zeros((BLOCK, LANES), F32)
 
+    core_order = (16 + (1 - xh) * 8, 0, 8, 16 + xh * 8)
+
     def core_send(c):
-        return push(R[c].at[pl.ds((1 - core) * 32, 32)], CX[c], at(core=1 - core))
-
-    def core_add(c, copy):
-        copy.wait_recv()
-
-        def body(q, carry):
-            for u in range(4):
-                b = q * 4 + u
+        return [
+            push(R[c].at[pl.ds((1 - core) * 32 + n, 8)], CX[c].at[pl.ds(n, 8)], at(core=1 - core))
+            for n in core_order
+        ]
+
+    def core_add(c, copies, parts):
+        for p in parts:
+            copies[p].wait_recv()
+            for u in range(8):
+                b = core_order[p] + u
                 T[c][b] = (R[c][core * 32 + b].astype(F32) + CX[c][b].astype(F32)).astype(BF16)
-            return carry
-
-        lax.fori_loop(0, 8, body, 0)
+
+    def core_start(c, copies):
+        core_add(c, copies, (0,))
+        b_pair = sum_start_pair(COL[c], T[c], z, xh, col_pair)
+        core_add(c, copies, (1, 2))
+        a_ring = sum_start_ring(COL[c], T[c], z, col_ring)
+        core_add(c, copies, (3,))
+        return b_pair, a_ring
 
     def activate(c, blocks):
         lanes = slice(c * LANES, (c + 1) * LANES)
@@ -245,7 +265,7 @@
             precision=lax.Precision.HIGHEST, preferred_element_type=F32,
         )
         for i in range(8):
-            WP[c][i, 32:40] = terms[i * 8:(i + 1) * 8]
+            wp[i, c * 48 + 32:c * 48 + 40] = terms[i * 8:(i + 1) * 8]
 
     to_core = at(core=1 - core)
 
@@ -266,13 +286,20 @@
         b_pair.wait_recv()
         return a_ring, b_other, [share(c, z * 8, 8)]
 
-    def grad_finish(c, state):
+    def grad_part(c, half, copies):
+        out = []
+        for d, copy in zip(hops, copies):
+            copy.wait_recv()
+            out.append(share(c, (z + 4 - d) % 4 * 8 + half, 4))
+        return out
+
+    def grad_first(c, state):
         a_ring, b_other, cores = state
-        for half, copies in ((0, a_ring), (4, b_other)):
-            for d, copy in zip(hops, copies):
-                copy.wait_recv()
-                cores.append(share(c, (z + 4 - d) % 4 * 8 + half, 4))
-        arrive(cores)
+        return b_other, cores + grad_part(c, 0, a_ring)
+
+    def grad_second(c, state):
+        b_other, cores = state
+        return cores + grad_part(c, 4, b_other)
 
     def finish_hidden(c, blocks):
         lanes = slice(c * LANES, (c + 1) * LANES)
@@ -289,39 +316,55 @@
                 part = part + jnp.dot(PP[c][spot], xg_v[nodes], preferred_element_type=F32)
         part = part.T
         for i in range(8):
-            WP[c][i, 0:32] = part[i * 32:(i + 1) * 32]
+            wp[i, c * 48:c * 48 + 32] = part[i * 32:(i + 1) * 32]
+
+    def weight_send():
         return [
-            push(WP[c].at[(row + d) % 8], WR[c].at[d - 1], ((row + d) % 8, col))
-            for d in range(1, 8)
+            push(wp.at[(row + d) % 8], wr.at[d - 1], ((row + d) % 8, col)) for d in range(1, 8)
         ]
 
-    def weight_cols(c, copies):
+    def weight_cores(copies):
         arrive(copies)
-        total = WP[c][row]
+        total = wp[row]
         for d in range(7):
-            total = total + WR[c][d]
-        WS[c][...] = total
-        return [
-            push(WS[c], WC[c].at[d - 1], (row, (col + d) % 16)) for d in range(1, 16)
-        ]
-
-    def weight_rows(c, copies):
+            total = total + wr[d]
+        ws[...] = total
+        return push(ws.at[pl.ds((1 - core) * 48, 48)], wk, to_core)
+
+    chip = z * 2 + xh
+
+    def weight_chips(copy):
+        copy.wait_recv()
+        wc[7] = ws[pl.ds(core * 48, 48)] + wk[...]
+        out = []
+        for d in range(1, 8):
+            other = (chip + d) % 8
+            out.append(push(wc.at[7], wc.at[d - 1], at(z=other // 2, xh=other % 2)))
+        return out
+
+    def weight_back(copies):
         arrive(copies)
-        WC[c][15] = WS[c][...]
-        total = jnp.zeros((48, LANES), F32)
-        for j in range(16):
-            total = total + WC[c][(col + 15 - j) % 16]
-        WF[c][row, 0:32] = total[0:32] / 256.0
-        WF[c][row, 32:48] = total[32:48]
-        mine = WF[c].at[row]
+        total = wc[(chip + 7) % 8]
+        for j in range(1, 8):
+            total = total + wc[(chip + 7 - j) % 8]
+        mine = pl.ds(core * 48, 48)
+        wf[row, mine] = total
+        half = wf.at[row, mine]
+        return push(half, half, to_core)
+
+    def weight_rows(copy):
+        copy.wait_recv()
+        mine = wf.at[row]
         return [push(mine, mine, ((row + d) % 8, col)) for d in range(1, 8)]
 
-    def weight_out(c, copies):
+    def weight_out(copies):
         arrive(copies)
-        lanes = slice(c * LANES, (c + 1) * LANES)
-        for i in range(8):
-            wg_ref[i * 32:(i + 1) * 32, lanes] = WF[c][i, 0:32]
-            gg_ref[i * 8:(i + 1) * 8, lanes] = WF[c][i, 32:40] / jnp.sqrt(WF[c][i, 40:48])
+        for c in range(CHUNKS):
+            lanes = slice(c * LANES, (c + 1) * LANES)
+            n = c * 48
+            for i in range(8):
+                wg_ref[i * 32:(i + 1) * 32, lanes] = wf[i, n:n + 32] / 256.0
+                gg_ref[i * 8:(i + 1) * 8, lanes] = wf[i, n + 32:n + 40] / jnp.sqrt(wf[i, n + 40:n + 48])
 
     gs0 = gather_start(H[0], 0, y, xl, row_ring, row_pair)
     for load in loads:
@@ -365,75 +408,80 @@
     acc = tile_pass(0, True, 0, 160, zero)
     ga1 = gather_on_pair(H[1], 0, y, row_ring, gs1[0])
     acc = tile_pass(0, True, 160, 256, acc)
-    gb1 = gather_on_ring(H[1], 0, y, xl, row_pair, gs1[1])
+    gb1 = gather_second(H[1], 0, y, xl, row_ring, gs1[2])
     tile_pass(0, True, 256, SLOTS, acc)
-    collect(R[0], 2, 64)
+    collect(R[0], 2, (1 - core) * 32)
     cs0 = core_send(0)
+    collect(R[0], 2, core * 32)
     sizes = jnp.dot(mt_v[...], jnp.ones((4 * BLOCK, LANES), F32), preferred_element_type=F32)
     for c in range(CHUNKS):
         for i in range(8):
-            WP[c][i, 40:48] = sizes[i * 8:(i + 1) * 8]
+            wp[i, c * 48 + 40:c * 48 + 48] = sizes[i * 8:(i + 1) * 8]
+    bp0, ar0 = core_start(0, cs0)
     rg_v[...] = lax.dot_general(
         mt_v[...], pg_ref[...], (((0,), (0,)), ((), ())),
         precision=lax.Precision.HIGHEST, preferred_element_type=F32,
     )
-    core_add(0, cs0)
-    bp0, ar0 = sum_start(COL[0], T[0], z, xh, col_ring, col_pair)
-    arrive(ga1 + gb1 + [gs1[2]])
+    arrive(ga1 + gb1 + gs1[1])
     own_x = xg_v.at[pl.ds(row * 512, 512)]
+    rx = [push(own_x, own_x, row_ring(d)) for d in hops]
+    acc = tile_pass(1, True, 0, 96, zero)
+    br0 = sum_on_pair(COL[0], T[0], z, xh, col_ring, bp0)
     px = push(own_x, own_x, row_pair)
-    rx = [push(own_x, own_x, row_ring(d)) for d in hops]
-    acc = tile_pass(1, True, 0, 128, zero)
-    br0 = sum_on_pair(COL[0], T[0], z, xh, col_ring, bp0)
-    tile_pass(1, True, 128, SLOTS, acc)
-    collect(R[1], 2, 64)
+    tile_pass(1, True, 96, SLOTS, acc)
+    collect(R[1], 2, (1 - core) * 32)
     cs1 = core_send(1)
+    collect(R[1], 2, core * 32)
     ap0 = sum_on_ring(COL[0], T[0], z, xh, col_pair, ar0)
-    core_add(1, cs1)
-    bp1, ar1 = sum_start(COL[1], T[1], z, xh, col_ring, col_pair)
+    bp1, ar1 = core_start(1, cs1)
     held0 = activate(0, sum_finish(COL[0], T[0], z, xh, br0, ap0))
     gg0 = grad_start(0)
+    br1 = sum_on_pair(COL[1], T[1], z, xh, col_ring, bp1)
+    gg0 = grad_on_pair(0, gg0)
     px.wait_recv()
     other_x = xg_v.at[pl.ds(((1 - xl) * 4 + y) * 512, 512)]
     rx += [push(other_x, other_x, row_ring(d)) for d in hops]
-    br1 = sum_on_pair(COL[1], T[1], z, xh, col_ring, bp1)
-    gg0 = grad_on_pair(0, gg0)
-    after_activate(0, held0)
     gg0 = grad_on_ring(0, gg0)
     ap1 = sum_on_ring(COL[1], T[1], z, xh, col_pair, ar1)
+    after_activate(0, held0)
     held1 = activate(1, sum_finish(COL[1], T[1], z, xh, br1, ap1))
     gg1 = grad_start(1)
-    grad_finish(0, gg0)
+    gg0 = grad_first(0, gg0)
     gg1 = grad_on_pair(1, gg1)
-    acc = tile_pass(0, False, 0, 96, zero)
+    gg0 = grad_second(0, gg0)
+    arrive(gg0)
+    acc = tile_pass(0, False, 0, 64, zero)
     gg1 = grad_on_ring(1, gg1)
-    tile_pass(0, False, 96, SLOTS, acc)
-    collect(PP[0], 3, 32)
-    bq0, aq0 = sum_start(ROW[0], PP[0], y, xl, row_ring, row_pair)
+    acc = tile_pass(0, False, 64, 256, acc)
+    gg1 = grad_first(1, gg1)
+    tile_pass(0, False, 256, SLOTS, acc)
+    collect(PP[0], 3, 0)
+    bq0, aq0 = row_start(0)
+    gg1 = grad_second(1, gg1)
+    arrive(rx)
     after_activate(1, held1)
-    arrive(rx)
-    grad_finish(1, gg1)
+    arrive(gg1)
     acc = tile_pass(1, False, 0, 128, zero)
     dq0 = sum_on_pair(ROW[0], PP[0], y, xl, row_ring, bq0)
-    acc = tile_pass(1, False, 128, SLOTS, acc)
-    collect(PP[1], 3, 32)
-    bq1, aq1 = sum_start(ROW[1], PP[1], y, xl, row_ring, row_pair)
+    tile_pass(1, False, 128, SLOTS, acc)
+    collect(PP[1], 3, 0)
+    bq1, aq1 = row_start(1)
+    weight_part(1)
+    weight_part(0)
+    sent = weight_send()
     eq0 = sum_on_ring(ROW[0], PP[0], y, xl, row_pair, aq0)
-    wr0_ = weight_part(0)
-    wr1_ = weight_part(1)
+    dq1 = sum_on_pair(ROW[1], PP[1], y, xl, row_ring, bq1)
+    crossed = weight_cores(sent)
     finish_hidden(0, sum_finish(ROW[0], PP[0], y, xl, dq0, eq0))
-    dq1 = sum_on_pair(ROW[1], PP[1], y, xl, row_ring, bq1)
-    wc0_ = weight_cols(0, wr0_)
-    wc1_ = weight_cols(1, wr1_)
+    passed = weight_chips(crossed)
     eq1 = sum_on_ring(ROW[1], PP[1], y, xl, row_pair, aq1)
-    wf0_ = weight_rows(0, wc0_)
-    wf1_ = weight_rows(1, wc1_)
+    crossed = weight_back(passed)
+    passed = weight_rows(crossed)
     finish_hidden(1, sum_finish(ROW[1], PP[1], y, xl, dq1, eq1))
     fg_ref[...] = lax.dot_general(
         hg_v[...], w_ref[...], (((1,), (1,)), ((), ())), preferred_element_type=F32
     ).astype(BF16)
-    weight_out(0, wf0_)
-    weight_out(1, wf1_)
+    weight_out(passed)
     for copy in started:
         copy.wait_send()
 
@@ -460,7 +508,7 @@
         *pair((3, 4) + tile), *pair((8,) + tile), *pair((8,) + tile),
         *pair((3, 2) + tile), *pair((2,) + tile), *pair((2,) + tile),
     ]
-    copies = 176
+    copies = 2 * 55 + 7 + 23
     outs = (
         jax.ShapeDtypeStruct((nodes, WIDTH), BF16),
         jax.ShapeDtypeStruct((nodes, WIDTH), BF16),
@@ -480,8 +528,9 @@
             *pair((32,) + tile), *pair((64,) + tile), *pair((32,) + tile), *pair((32,) + tile),
             *pair((64,) + tile), *pair((32,) + tile),
             *sums, *sums,
-            *pair((8, 48, LANES), F32), *pair((7, 48, LANES), F32), *pair((48, LANES), F32),
-            *pair((16, 48, LANES), F32), *pair((8, 48, LANES), F32),
+            pltpu.VMEM((8, 96, LANES), F32), pltpu.VMEM((7, 96, LANES), F32),
+            pltpu.VMEM((96, LANES), F32), pltpu.VMEM((48, LANES), F32),
+            pltpu.VMEM((8, 48, LANES), F32), pltpu.VMEM((8, 96, LANES), F32),
             pltpu.VMEM((nodes, WIDTH), F32),
             pltpu.VMEM((PARTS, nodes), F32),
             pltpu.VMEM((8 * nodes, WIDTH), BF16),

time: 118 us -> 117 us (level)
  Pallas kernels: 117 us -> 115 us
where the time goes in v4:
time: 117 us
  Pallas kernels  115 us (98%)
  between operations  1.29 us (1%)
    pallas_call x1, Pallas kernels, per_device(): pl.pallas_call(kernel, out_shape=outs, in_specs=[vmem, vmem, smem, vmem,...  113 us

profile of v4, /device:TPU:1, one launch (start us, length us, event | category | flops | bytes accessed | tf_op | source)
XLA Modules:
  0.0 116.7 jit_solution(6368452021198894804)
XLA Ops:
  1.3 113.4 %shard_map.120 = (bf16[512,256]{1,0:T(8,128)(2,1)}, bf16[512,256]{1,0:T(8,128)(2,1)}, f32[256,256]{1,0:T(8,128)}, f32[64,256]{1,0:T(8,128)}) custom-call(s32[1,384]{1,0:T(1,128)} %bitcast.6, s32[1,384]{1,0:T(1,128)} %bitcast.7, s32[1,1]{1,0:T(1,128)S(6)} %copy.13.live_ref, bf16[512,256]{1,0:T(8,128)(2,1)} %x_ref.1, bf16[256,256]{1,0:T(8,128)(2,1)} %w_ref.1, ...), custom_call_target="tpu_custom_call" | custom-call | tf_op jit(solution)/shard_map/pallas_call | solution.py:518
  114.6 2.0 %shard_map.121 = (bf16[512,256]{1,0:T(8,128)(2,1)}, bf16[512,256]{1,0:T(8,128)(2,1)}, f32[256,256]{1,0:T(8,128)}, f32[64,256]{1,0:T(8,128)}) custom-call(bf16[512,256]{1,0:T(8,128)(2,1)} %get-tuple-element.8.refs_0_, bf16[512,256]{1,0:T(8,128)(2,1)} %get-tuple-element.9.refs_1_, f32[256,256]{1,0:T(8,128)} %get-tuple-element.10.refs_2_, ...), custom_call_target="tpu_custom_call" | custom-call | tf_op jit(solution)/shard_map/pallas_call | solution.py:550

commit v5 on v4

--- a/solution.py
+++ b/solution.py
@@ -285,6 +285,13 @@
         b_other = gather_on_ring(G[c], core * 32, z, xh, col_pair, b_ring)
         b_pair.wait_recv()
         return a_ring, b_other, [share(c, z * 8, 8)]
+
+    def grad_on_ring_light(c, state):
+        a_ring, b_ring, b_pair = state
+        b_other = gather_second(G[c], core * 32, z, xh, col_ring, b_pair)
+        cores = [share(c, z * 8, 8)]
+        arrive(b_ring)
+        return a_ring, b_other, cores
 
     def grad_part(c, half, copies):
         out = []
@@ -451,7 +458,7 @@
     gg0 = grad_second(0, gg0)
     arrive(gg0)
     acc = tile_pass(0, False, 0, 64, zero)
-    gg1 = grad_on_ring(1, gg1)
+    gg1 = grad_on_ring_light(1, gg1)
     acc = tile_pass(0, False, 64, 256, acc)
     gg1 = grad_first(1, gg1)
     tile_pass(0, False, 256, SLOTS, acc)

time: 117 us -> 118 us (level)
  Pallas kernels: 115 us -> 117 us
    pallas_call x1, Pallas kernels: 113 us -> 115 us  [per_device(): pl.pallas_call(kernel, out_shape=outs, in_specs=[vmem, vmem, smem, vmem,...]
where the time goes in v5:
time: 118 us
  Pallas kernels  117 us (99%)
  between operations  1.29 us (1%)
    pallas_call x1, Pallas kernels, per_device(): pl.pallas_call(kernel, out_shape=outs, in_specs=[vmem, vmem, smem, vmem,...  115 us

profile of v5, /device:TPU:1, one launch (start us, length us, event | category | flops | bytes accessed | tf_op | source)
XLA Modules:
  0.0 118.1 jit_solution(1639203693262344156)
XLA Ops:
  1.3 114.8 %shard_map.120 = (bf16[512,256]{1,0:T(8,128)(2,1)}, bf16[512,256]{1,0:T(8,128)(2,1)}, f32[256,256]{1,0:T(8,128)}, f32[64,256]{1,0:T(8,128)}) custom-call(s32[1,384]{1,0:T(1,128)} %bitcast.6, s32[1,384]{1,0:T(1,128)} %bitcast.7, s32[1,1]{1,0:T(1,128)S(6)} %copy.13.live_ref, bf16[512,256]{1,0:T(8,128)(2,1)} %x_ref.1, bf16[256,256]{1,0:T(8,128)(2,1)} %w_ref.1, ...), custom_call_target="tpu_custom_call" | custom-call | tf_op jit(solution)/shard_map/pallas_call | solution.py:525
  116.1 2.0 %shard_map.121 = (bf16[512,256]{1,0:T(8,128)(2,1)}, bf16[512,256]{1,0:T(8,128)(2,1)}, f32[256,256]{1,0:T(8,128)}, f32[64,256]{1,0:T(8,128)}) custom-call(bf16[512,256]{1,0:T(8,128)(2,1)} %get-tuple-element.8.refs_0_, bf16[512,256]{1,0:T(8,128)(2,1)} %get-tuple-element.9.refs_1_, f32[256,256]{1,0:T(8,128)} %get-tuple-element.10.refs_2_, ...), custom_call_target="tpu_custom_call" | custom-call | tf_op jit(solution)/shard_map/pallas_call | solution.py:557
